TPU v7x, 32 devices: a whole 2x2x4 slice. The times are simulated.
32 devices in a mesh: groups: 2 (over y), tm: 4 (over z), lat: 2 (over x), lon: 2 (over core).
Axes of the slice: x: 2, y: 2, z: 4, core: 2. Of those that a mesh axis runs over, the one named last changes fastest.
Arguments:
- prior_state: float32 [16, 8, 16, 256], P(('groups', 'tm'), None, 'lat', 'lon'), parts along dimension 0, may hold values from -6 to 6
- observed: float32 [16, 8, 16, 256], P(('groups', 'tm'), None, 'lat', 'lon'), parts along dimension 0, may hold values from -6 to 6
- obs_weight: float32 [16, 8, 16, 256], P(('groups', 'tm'), None, 'lat', 'lon'), parts along dimension 0, may hold values from 0 to 2
- noise_field: float32 [2, 16, 8, 16, 256], P(None, ('groups', 'tm'), None, 'lat', 'lon'), parts along dimension 1, may hold values from -6 to 6
- step_sizes: float32 [2], replicated, may hold values from 0.05 to 0.3
- lift_weight: float32 [96, 40], replicated, may hold values from -1 to 1
- conv_weights: bfloat16 [2, 9, 96, 96], replicated, may hold values from -0.21875 to 0.21875
- out_weight: bfloat16 [8, 96], replicated, may hold values from -0.625 to 0.625
Outputs:
- analysis: float32 [16, 8, 16, 256], P(('groups', 'tm'), None, 'lat', 'lon'), parts along dimension 0
There are 2 independent parts, one for each index of `groups`. A program takes and returns all parts, laid end to end along the dimension named above; an argument that names none is the same for every part. Nothing has to cross between parts.
All inputs are finite; a program needn't handle non-finite values.
Results may differ from a plain program's by a relative error of at most 0.0012.
Values may be sent and summed in bfloat16 or wider, within the bound.
No kernel may reach another device: no remote copies, remote signals or barrier semaphores. Data moves between devices by JAX's collectives and lax.ppermute only.
A program may use at most 64 MiB of HBM per device.

v0:
```python
import jax
import jax.numpy as jnp
from jax import lax
from jax.sharding import PartitionSpec as P


def extended_2(block, sides, width, periodic):
    for axis, dim in sides:
        count = lax.axis_size(axis)
        forward = [(i, i + 1) for i in range(count - 1)]
        if periodic:
            forward.append((count - 1, 0))
        backward = [(target, source) for source, target in forward]
        low = lax.ppermute(
            lax.slice_in_dim(block, block.shape[dim] - width, None, axis=dim), axis, forward
        )
        high = lax.ppermute(lax.slice_in_dim(block, 0, width, axis=dim), axis, backward)
        block = jnp.concatenate([low, block, high], axis=dim)
    return block


def rim_rows(values, margin):
    row_count = values.shape[2]
    own_rows = row_count - 2 * margin
    row_start = lax.axis_index("lat") * own_rows - margin
    row_index = row_start + lax.iota(jnp.int32, row_count)
    inside = (row_index >= 0) & (row_index < own_rows * lax.axis_size("lat"))
    return values * inside.astype(values.dtype)[None, None, :, None]


def conv_valid(values, kernel):
    row_count = values.shape[2] - 2
    col_count = values.shape[3] - 2
    summed = jnp.zeros((values.shape[0], kernel.shape[1], row_count, col_count), jnp.float32)
    for row_off in range(3):
        for col_off in range(3):
            part = values[:, :, row_off : row_off + row_count, col_off : col_off + col_count]
            summed = summed + jnp.einsum(
                "oi,firw->forw",
                kernel[3 * row_off + col_off],
                part,
                preferred_element_type=jnp.float32,
            )
    return summed


def wide_border(values):
    return rim_rows(extended_2(values, (("lat", 2), ("lon", 3)), 2, True), 2)


def score_all(current, lift_weight, conv_weights, out_weight):
    frame_count = current.shape[0]
    extended = extended_2(current, (("tm", 0),), 2, False)
    stacked = jnp.concatenate(
        [extended[offset : offset + frame_count] for offset in range(5)], axis=1
    )
    lifted = jnp.einsum(
        "oc,fcrw->forw", lift_weight, stacked, precision=lax.Precision.HIGHEST
    ).astype(jnp.bfloat16)
    activated = jax.nn.silu(conv_valid(wide_border(lifted), conv_weights[0])).astype(jnp.bfloat16)
    activated = rim_rows(activated, 1)
    second = jax.nn.silu(conv_valid(activated, conv_weights[1]))
    merged = (lifted.astype(jnp.float32) + second).astype(jnp.bfloat16)
    return jnp.einsum("co,forw->fcrw", out_weight, merged, preferred_element_type=jnp.float32)


def per_device(
    prior_state,
    observed,
    obs_weight,
    noise_field,
    step_sizes,
    lift_weight,
    conv_weights,
    out_weight,
):
    current = prior_state
    for update in range(noise_field.shape[0]):
        step_size = step_sizes[update]
        score = score_all(current, lift_weight, conv_weights, out_weight)
        current = (
            current
            + step_size * (score + obs_weight * (observed - current))
            + jnp.sqrt(2.0 * step_size) * noise_field[update]
        )
    return current


def solution(mesh):
    placed = (
        P(("groups", "tm"), None, "lat", "lon"),
        P(("groups", "tm"), None, "lat", "lon"),
        P(("groups", "tm"), None, "lat", "lon"),
        P(None, ("groups", "tm"), None, "lat", "lon"),
        P(),
        P(),
        P(),
        P(),
    )
    return jax.shard_map(
        per_device,
        mesh=mesh,
        in_specs=placed,
        out_specs=P(("groups", "tm"), None, "lat", "lon"),
        check_vma=False,
    )
```

profile of v0, /device:TPU:0, one launch (start us, length us, event | category | flops | bytes accessed | tf_op | source)
XLA Modules:
  0.0 66.9 jit_solution(1176170069174629272)
XLA Ops:
  0.0 0.9 %copy.89 = f32[2,8,8,128]{3,1,2,0:T(8,128)S(1)} copy(f32[2,8,8,128]{3,2,1,0:T(8,128)} %param.8) | data formatting | bytes 131072 | tf_op args[0]
  0.9 5.0 %collective-permute-start = (f32[2,8,8,128]{3,1,2,0:T(8,128)S(1)}, f32[2,8,8,128]{3,1,2,0:T(8,128)S(1)}, u32[]{:S(2)}, u32[]{:S(2)}) collective-permute-start(f32[2,8,8,128]{3,1,2,0:T(8,128)S(1)} %copy.89), channel_id=1, source_target_pairs={{0,4},{4,8},{8,12},{1,5},{5,9},{9,13},{2,6},{6,10},{10,14},{3,7},{... | collective-permute-start | bytes 196616 | tf_op jit(solution)/shard_map/ppermute | solution.py:14
  5.8 1.3 %collective-permute-start.1 = (f32[2,8,8,128]{3,1,2,0:T(8,128)S(1)}, f32[2,8,8,128]{3,1,2,0:T(8,128)S(1)}, u32[]{:S(2)}, u32[]{:S(2)}) collective-permute-start(f32[2,8,8,128]{3,1,2,0:T(8,128)S(1)} %copy.89), channel_id=1, source_target_pairs={{4,0},{8,4},{12,8},{5,1},{9,5},{13,9},{6,2},{10,6},{14,10},{7,3},{... | collective-permute-start | bytes 196616 | tf_op jit(solution)/shard_map/ppermute | solution.py:17
  7.1 0.9 %fusion.158 = (f32[1,2,8,8,128]{4,3,2,1,0:T(8,128)S(1)}, f32[1,2,8,8,128]{4,3,2,1,0:T(8,128)S(1)}) fusion(f32[2,2,8,8,128]{4,3,2,1,0:T(8,128)} %param.11), kind=kLoop, calls=%fused_computation.204 | loop fusion | bytes 262144 | tf_op jit(solution)/shard_map/slice | solution.py:84
  8.0 1.3 %fusion.159 = (f32[1]{0:T(128)}, f32[1]{0:T(128)}) fusion(f32[2]{0:T(128)} %param.12), kind=kLoop, calls=%fused_computation.205 | loop fusion | bytes 16 | tf_op jit(solution)/shard_map/slice | solution.py:79
  9.4 0.9 %constant_dynamic-update-slice_fusion.1 = f32[2,40,8,128]{3,1,2,0:T(8,128)S(1)} fusion(f32[2,40,8,128]{3,1,2,0:T(8,128)S(1)} %fusion.69, f32[2,8,8,128]{3,2,1,0:T(8,128)} %param.8), kind=kLoop, calls=%fused_computation.151 | loop fusion | bytes 131072
  10.2 1.8 %collective-permute-done.1 = f32[2,8,8,128]{3,1,2,0:T(8,128)S(1)} collective-permute-done((f32[2,8,8,128]{3,1,2,0:T(8,128)S(1)}, f32[2,8,8,128]{3,1,2,0:T(8,128)S(1)}, u32[]{:S(2)}, u32[]{:S(2)}) %collective-permute-start.1) | collective-permute-done | bytes 65568 | tf_op jit(solution)/shard_map/ppermute | solution.py:17
  12.0 0.8 %fusion.4 = bf16[2,96,8,128]{3,1,2,0:T(8,128)(2,1)S(1)} fusion(f32[2,40,8,128]{3,1,2,0:T(8,128)S(1)} %constant_dynamic-update-slice_fusion, f32[96,40]{0,1:T(8,128)S(1)} %copy-done), kind=kOutput, calls=%fused_computation.40 | convolution fusion | flops 94568448 | bytes 736256 | tf_op jit(solution)/shard_map/oc,fcrw->forw/dot_general | solution.py:57
  12.9 1.6 %collective-permute-start.2 = (bf16[2,96,2,128]{3,1,2,0:T(8,128)(2,1)S(1)}, bf16[2,96,2,128]{3,1,2,0:T(8,128)(2,1)S(1)}, u32[]{:S(2)}, u32[]{:S(2)}) collective-permute-start(bf16[2,96,2,128]{3,1,2,0:T(8,128)(2,1)S(1)} %get-tuple-element.11), channel_id=1, source_target_pairs={{0,2},{2,0},{1,3},{3,1},{4,6},{6,4},{5,7},{7,5},{8,10},{10,8},{9,1... | collective-permute-start | bytes 294920 | tf_op jit(solution)/shard_map/ppermute | solution.py:14
  14.4 0.5 collective-permute-start.3
  15.0 2.6 %collective-permute-done.2 = bf16[2,96,2,128]{3,1,2,0:T(8,128)(2,1)S(1)} collective-permute-done((bf16[2,96,2,128]{3,1,2,0:T(8,128)(2,1)S(1)}, bf16[2,96,2,128]{3,1,2,0:T(8,128)(2,1)S(1)}, u32[]{:S(2)}, u32[]{:S(2)}) %collective-permute-start.2) | collective-permute-done | bytes 98336 | tf_op jit(solution)/shard_map/ppermute | solution.py:14
  17.6 1.5 %collective-permute-done.3 = bf16[2,96,2,128]{3,1,2,0:T(8,128)(2,1)S(1)} collective-permute-done((bf16[2,96,2,128]{3,1,2,0:T(8,128)(2,1)S(1)}, bf16[2,96,2,128]{3,1,2,0:T(8,128)(2,1)S(1)}, u32[]{:S(2)}, u32[]{:S(2)}) %collective-permute-start.3) | collective-permute-done | bytes 98336 | tf_op jit(solution)/shard_map/ppermute | solution.py:17
  20.0 0.5 collective-permute-start.5
  21.9 0.8 %maximum_multiply_fusion = bf16[2,96,12,132]{3,1,2,0:T(8,128)(2,1)S(1)} fusion(bf16[2,96,12,2]{3,1,2,0:T(8,128)(2,1)S(1)} %copy.67, bf16[2,96,2,128]{3,1,2,0:T(8,128)(2,1)S(1)} %collective-permute-done.3, bf16[2,96,8,128]{3,1,2,0:T(8,128)(2,1)S(1)} %fusion.4, bf16[2,96,2,128]{3,1,2,0:T(8,128)(2,1)S(1)} %collective-permute-done.2, ...), kind=kLoop, calls=%fused_computation.44 | loop fusion | flops 3649536 | bytes 1216536 | tf_op jit(solution)/shard_map/mul | solution.py:28
  22.9 0.6 fusion.34
  23.5 1.0 %convolution_add_fusion.15 = f32[2,10,130,96]{3,2,1,0:T(8,128)S(1)} fusion(f32[2,10,130,96]{3,2,1,0:T(8,128)S(1)} %fusion.34, bf16[2,96,12,132]{3,1,2,0:T(8,128)(2,1)S(1)} %maximum_multiply_fusion, bf16[2,9,96,96]{3,2,1,0:T(8,128)(2,1)S(1)} %copy-done.1), kind=kOutput, calls=%fused_computation.17 | convolution fusion | flops 48172800 | bytes 3398656 | tf_op jit(solution)/shard_map/oi,firw->forw/dot_general | solution.py:38
  24.5 1.0 %convolution_add_fusion.14 = f32[2,10,130,96]{3,2,1,0:T(8,128)S(1)} fusion(f32[2,10,130,96]{3,2,1,0:T(8,128)S(1)} %convolution_add_fusion.15, bf16[2,96,12,132]{3,1,2,0:T(8,128)(2,1)S(1)} %maximum_multiply_fusion, bf16[2,9,96,96]{3,2,1,0:T(8,128)(2,1)S(1)} %copy-done.1), kind=kOutput, calls=%fused_computation.16 | convolution fusion | flops 48172800 | bytes 3398656 | tf_op jit(solution)/shard_map/oi,firw->forw/dot_general | solution.py:38
  25.4 0.6 convolution_add_fusion.13
  26.0 1.0 %convolution_add_fusion.12 = f32[2,10,130,96]{3,2,1,0:T(8,128)S(1)} fusion(f32[2,10,130,96]{3,2,1,0:T(8,128)S(1)} %convolution_add_fusion.13, bf16[2,96,12,132]{3,1,2,0:T(8,128)(2,1)S(1)} %maximum_multiply_fusion, bf16[2,9,96,96]{3,2,1,0:T(8,128)(2,1)S(1)} %copy-done.1), kind=kOutput, calls=%fused_computation.14 | convolution fusion | flops 48172800 | bytes 3398656 | tf_op jit(solution)/shard_map/oi,firw->forw/dot_general | solution.py:38
  27.0 1.0 %convolution_add_fusion.11 = f32[2,10,130,96]{3,2,1,0:T(8,128)S(1)} fusion(f32[2,10,130,96]{3,2,1,0:T(8,128)S(1)} %convolution_add_fusion.12, bf16[2,96,12,132]{3,1,2,0:T(8,128)(2,1)S(1)} %maximum_multiply_fusion, bf16[2,9,96,96]{3,2,1,0:T(8,128)(2,1)S(1)} %copy-done.1), kind=kOutput, calls=%fused_computation.13 | convolution fusion | flops 48172800 | bytes 3398656 | tf_op jit(solution)/shard_map/oi,firw->forw/dot_general | solution.py:38
  27.9 0.6 convolution_add_fusion.10
  28.5 1.0 %convolution_add_fusion.9 = f32[2,10,130,96]{3,2,1,0:T(8,128)S(1)} fusion(f32[2,10,130,96]{3,2,1,0:T(8,128)S(1)} %convolution_add_fusion.10, bf16[2,96,12,132]{3,1,2,0:T(8,128)(2,1)S(1)} %maximum_multiply_fusion, bf16[2,9,96,96]{3,2,1,0:T(8,128)(2,1)S(1)} %copy-done.1), kind=kOutput, calls=%fused_computation.11 | convolution fusion | flops 48172800 | bytes 3398656 | tf_op jit(solution)/shard_map/oi,firw->forw/dot_general | solution.py:38
  29.5 1.0 %fusion.6 = bf16[2,96,10,130]{1,3,2,0:T(8,128)(2,1)S(1)} fusion(f32[2,10,130,96]{3,2,1,0:T(8,128)S(1)} %convolution_add_fusion.9, bf16[2,96,12,132]{3,1,2,0:T(8,128)(2,1)S(1)} %maximum_multiply_fusion, bf16[10]{0:T(256)(128)(2,1)S(1)} %and_convert_fusion, bf16[2,9,96,96]{3,2,1,0:T(8,128)(2,1)S(1)} %copy-done.1), kind=kOutput, calls=%fused_computation.42 | convolution fusion | flops 49670400 | bytes 2899968 | tf_op jit(solution)/shard_map/oi,firw->forw/dot_general | solution.py:38
  33.1 0.5 copy-done.2
  33.6 1.2 %fusion.14 = f32[2,8,8,128]{3,1,2,0:T(8,128)S(1)} fusion(bf16[2,96,8,128]{3,1,2,0:T(8,128)(2,1)S(1)} %fusion.4, f32[2,8,128,96]{2,3,1,0:T(8,128)S(1)} %convolution_add_fusion.25, bf16[2,96,10,130]{1,3,2,0:T(8,128)(2,1)S(1)} %fusion.6, f32[1,2,8,8,128]{4,3,2,1,0:T(8,128)S(1)} %get-tuple-element.14, f32[2,8,8,128]{3,2,1,0:T(8,128)S(1)} %copy-done.3, ...), kind=kOutput, calls=%fused_computation.54 | convolution fusion | flops 42582016 | bytes 2058248 | tf_op jit(solution)/shard_map/co,forw->fcrw/dot_general | solution.py:64
  34.8 3.7 %collective-permute-start.6 = (f32[2,8,8,128]{3,1,2,0:T(8,128)S(1)}, f32[2,8,8,128]{3,1,2,0:T(8,128)S(1)}, u32[]{:S(2)}, u32[]{:S(2)}) collective-permute-start(f32[2,8,8,128]{3,1,2,0:T(8,128)S(1)} %fusion.14), channel_id=1, source_target_pairs={{0,4},{4,8},{8,12},{1,5},{5,9},{9,13},{2,6},{6,10},{10,14},{3,7},{... | collective-permute-start | bytes 196616 | tf_op jit(solution)/shard_map/ppermute | solution.py:14
  38.5 1.3 %collective-permute-start.7 = (f32[2,8,8,128]{3,1,2,0:T(8,128)S(1)}, f32[2,8,8,128]{3,1,2,0:T(8,128)S(1)}, u32[]{:S(2)}, u32[]{:S(2)}) collective-permute-start(f32[2,8,8,128]{3,1,2,0:T(8,128)S(1)} %fusion.14), channel_id=1, source_target_pairs={{4,0},{8,4},{12,8},{5,1},{9,5},{13,9},{6,2},{10,6},{14,10},{7,3},{... | collective-permute-start | bytes 196616 | tf_op jit(solution)/shard_map/ppermute | solution.py:17
  39.8 0.6 collective-permute-done.6
  40.4 4.2 %collective-permute-done.7 = f32[2,8,8,128]{3,1,2,0:T(8,128)S(1)} collective-permute-done((f32[2,8,8,128]{3,1,2,0:T(8,128)S(1)}, f32[2,8,8,128]{3,1,2,0:T(8,128)S(1)}, u32[]{:S(2)}, u32[]{:S(2)}) %collective-permute-start.7) | collective-permute-done | bytes 65568 | tf_op jit(solution)/shard_map/ppermute | solution.py:17
  44.6 0.8 %fusion.5 = bf16[2,96,8,128]{3,1,2,0:T(8,128)(2,1)S(1)} fusion(f32[2,40,8,128]{3,1,2,0:T(8,128)S(1)} %constant_dynamic-update-slice_fusion.3, f32[96,40]{0,1:T(8,128)S(1)} %copy-done), kind=kOutput, calls=%fused_computation.41 | convolution fusion | flops 94568448 | bytes 736256 | tf_op jit(solution)/shard_map/oc,fcrw->forw/dot_general | solution.py:57
  45.5 1.1 %collective-permute-start.8 = (bf16[2,96,2,128]{3,1,2,0:T(8,128)(2,1)S(1)}, bf16[2,96,2,128]{3,1,2,0:T(8,128)(2,1)S(1)}, u32[]{:S(2)}, u32[]{:S(2)}) collective-permute-start(bf16[2,96,2,128]{3,1,2,0:T(8,128)(2,1)S(1)} %get-tuple-element.9), channel_id=1, source_target_pairs={{0,2},{2,0},{1,3},{3,1},{4,6},{6,4},{5,7},{7,5},{8,10},{10,8},{9,1... | collective-permute-start | bytes 294920 | tf_op jit(solution)/shard_map/ppermute | solution.py:14
  46.6 1.0 %collective-permute-start.9 = (bf16[2,96,2,128]{3,1,2,0:T(8,128)(2,1)S(1)}, bf16[2,96,2,128]{3,1,2,0:T(8,128)(2,1)S(1)}, u32[]{:S(2)}, u32[]{:S(2)}) collective-permute-start(bf16[2,96,2,128]{3,1,2,0:T(8,128)(2,1)S(1)} %get-tuple-element.10), channel_id=1, source_target_pairs={{2,0},{0,2},{3,1},{1,3},{6,4},{4,6},{7,5},{5,7},{10,8},{8,10},{11,... | collective-permute-start | bytes 294920 | tf_op jit(solution)/shard_map/ppermute | solution.py:17
  47.6 2.6 %collective-permute-done.8 = bf16[2,96,2,128]{3,1,2,0:T(8,128)(2,1)S(1)} collective-permute-done((bf16[2,96,2,128]{3,1,2,0:T(8,128)(2,1)S(1)}, bf16[2,96,2,128]{3,1,2,0:T(8,128)(2,1)S(1)}, u32[]{:S(2)}, u32[]{:S(2)}) %collective-permute-start.8) | collective-permute-done | bytes 98336 | tf_op jit(solution)/shard_map/ppermute | solution.py:14
  50.2 1.1 %collective-permute-done.9 = bf16[2,96,2,128]{3,1,2,0:T(8,128)(2,1)S(1)} collective-permute-done((bf16[2,96,2,128]{3,1,2,0:T(8,128)(2,1)S(1)}, bf16[2,96,2,128]{3,1,2,0:T(8,128)(2,1)S(1)}, u32[]{:S(2)}, u32[]{:S(2)}) %collective-permute-start.9) | collective-permute-done | bytes 98336 | tf_op jit(solution)/shard_map/ppermute | solution.py:17
  52.2 0.5 collective-permute-start.11
  53.4 0.4 copy.93
  54.1 0.8 %maximum_multiply_fusion.1 = bf16[2,96,12,132]{3,1,2,0:T(8,128)(2,1)S(1)} fusion(bf16[2,96,12,2]{3,1,2,0:T(8,128)(2,1)S(1)} %copy.94, bf16[2,96,2,128]{3,1,2,0:T(8,128)(2,1)S(1)} %collective-permute-done.9, bf16[2,96,8,128]{3,1,2,0:T(8,128)(2,1)S(1)} %fusion.5, bf16[2,96,2,128]{3,1,2,0:T(8,128)(2,1)S(1)} %collective-permute-done.8, ...), kind=kLoop, calls=%fused_computation.45 | loop fusion | flops 3649536 | bytes 1216536 | tf_op jit(solution)/shard_map/mul | solution.py:28
  55.0 0.6 fusion.24
  55.5 1.0 %convolution_add_fusion.7 = f32[2,10,130,96]{3,2,1,0:T(8,128)S(1)} fusion(f32[2,10,130,96]{3,2,1,0:T(8,128)S(1)} %fusion.24, bf16[2,96,12,132]{3,1,2,0:T(8,128)(2,1)S(1)} %maximum_multiply_fusion.1, bf16[2,9,96,96]{3,2,1,0:T(8,128)(2,1)S(1)} %copy-done.1), kind=kOutput, calls=%fused_computation.8 | convolution fusion | flops 48172800 | bytes 3398656 | tf_op jit(solution)/shard_map/oi,firw->forw/dot_general | solution.py:38
  56.5 1.0 %convolution_add_fusion.6 = f32[2,10,130,96]{3,2,1,0:T(8,128)S(1)} fusion(f32[2,10,130,96]{3,2,1,0:T(8,128)S(1)} %convolution_add_fusion.7, bf16[2,96,12,132]{3,1,2,0:T(8,128)(2,1)S(1)} %maximum_multiply_fusion.1, bf16[2,9,96,96]{3,2,1,0:T(8,128)(2,1)S(1)} %copy-done.1), kind=kOutput, calls=%fused_computation.7 | convolution fusion | flops 48172800 | bytes 3398656 | tf_op jit(solution)/shard_map/oi,firw->forw/dot_general | solution.py:38
  57.5 0.6 convolution_add_fusion.5
  58.0 1.0 %convolution_add_fusion.4 = f32[2,10,130,96]{3,2,1,0:T(8,128)S(1)} fusion(f32[2,10,130,96]{3,2,1,0:T(8,128)S(1)} %convolution_add_fusion.5, bf16[2,96,12,132]{3,1,2,0:T(8,128)(2,1)S(1)} %maximum_multiply_fusion.1, bf16[2,9,96,96]{3,2,1,0:T(8,128)(2,1)S(1)} %copy-done.1), kind=kOutput, calls=%fused_computation.5 | convolution fusion | flops 48172800 | bytes 3398656 | tf_op jit(solution)/shard_map/oi,firw->forw/dot_general | solution.py:38
  59.0 1.0 %convolution_add_fusion.3 = f32[2,10,130,96]{3,2,1,0:T(8,128)S(1)} fusion(f32[2,10,130,96]{3,2,1,0:T(8,128)S(1)} %convolution_add_fusion.4, bf16[2,96,12,132]{3,1,2,0:T(8,128)(2,1)S(1)} %maximum_multiply_fusion.1, bf16[2,9,96,96]{3,2,1,0:T(8,128)(2,1)S(1)} %copy-done.1), kind=kOutput, calls=%fused_computation.4 | convolution fusion | flops 48172800 | bytes 3398656 | tf_op jit(solution)/shard_map/oi,firw->forw/dot_general | solution.py:38
  60.0 0.6 convolution_add_fusion.2
  60.5 1.0 %convolution_add_fusion.1 = f32[2,10,130,96]{3,2,1,0:T(8,128)S(1)} fusion(f32[2,10,130,96]{3,2,1,0:T(8,128)S(1)} %convolution_add_fusion.2, bf16[2,96,12,132]{3,1,2,0:T(8,128)(2,1)S(1)} %maximum_multiply_fusion.1, bf16[2,9,96,96]{3,2,1,0:T(8,128)(2,1)S(1)} %copy-done.1), kind=kOutput, calls=%fused_computation.2 | convolution fusion | flops 48172800 | bytes 3398656 | tf_op jit(solution)/shard_map/oi,firw->forw/dot_general | solution.py:38
  61.5 1.0 %fusion.7 = bf16[2,96,10,130]{1,3,2,0:T(8,128)(2,1)S(1)} fusion(f32[2,10,130,96]{3,2,1,0:T(8,128)S(1)} %convolution_add_fusion.1, bf16[2,96,12,132]{3,1,2,0:T(8,128)(2,1)S(1)} %maximum_multiply_fusion.1, bf16[10]{0:T(256)(128)(2,1)S(1)} %and_convert_fusion, bf16[2,9,96,96]{3,2,1,0:T(8,128)(2,1)S(1)} %copy-done.1), kind=kOutput, calls=%fused_computation.43 | convolution fusion | flops 49670400 | bytes 2899968 | tf_op jit(solution)/shard_map/oi,firw->forw/dot_general | solution.py:38
  65.1 1.2 %fusion.15 = f32[2,8,8,128]{3,1,2,0:T(8,128)S(1)} fusion(f32[2,8,8,128]{3,1,2,0:T(8,128)S(1)} %fusion.14, bf16[2,96,8,128]{3,1,2,0:T(8,128)(2,1)S(1)} %fusion.5, f32[2,8,128,96]{2,3,1,0:T(8,128)S(1)} %convolution_add_fusion.17, bf16[2,96,10,130]{1,3,2,0:T(8,128)(2,1)S(1)} %fusion.7, f32[1,2,8,8,128]{4,3,2,1,0:T(8,128)S(1)} %get-tuple-element.13, ...), kind=kOutput, calls=%fused_computation.55 | convolution fusion | flops 42582016 | bytes 2058248 | tf_op jit(solution)/shard_map/co,forw->fcrw/dot_general | solution.py:64
  66.3 0.6 copy.116
  (58 shorter events, 8.3 us)
Async XLA Ops:
  0.0 12.0 %copy-start = (f32[96,40]{0,1:T(8,128)S(1)}, f32[96,40]{0,1:T(8,128)}, u32[]{:S(2)}) copy-start(f32[96,40]{0,1:T(8,128)} %param.13) | copy-start | bytes 46084
  0.9 8.5 %collective-permute-start = (f32[2,8,8,128]{3,1,2,0:T(8,128)S(1)}, f32[2,8,8,128]{3,1,2,0:T(8,128)S(1)}, u32[]{:S(2)}, u32[]{:S(2)}) collective-permute-start(f32[2,8,8,128]{3,1,2,0:T(8,128)S(1)} %copy.89), channel_id=1, source_target_pairs={{0,4},{4,8},{8,12},{1,5},{5,9},{9,13},{2,6},{6,10},{10,14},{3,7},{... | collective-permute-start | bytes 196616 | tf_op jit(solution)/shard_map/ppermute | solution.py:14
  5.8 6.2 %collective-permute-start.1 = (f32[2,8,8,128]{3,1,2,0:T(8,128)S(1)}, f32[2,8,8,128]{3,1,2,0:T(8,128)S(1)}, u32[]{:S(2)}, u32[]{:S(2)}) collective-permute-start(f32[2,8,8,128]{3,1,2,0:T(8,128)S(1)} %copy.89), channel_id=1, source_target_pairs={{4,0},{8,4},{12,8},{5,1},{9,5},{13,9},{6,2},{10,6},{14,10},{7,3},{... | collective-permute-start | bytes 196616 | tf_op jit(solution)/shard_map/ppermute | solution.py:17
  12.9 4.7 %collective-permute-start.2 = (bf16[2,96,2,128]{3,1,2,0:T(8,128)(2,1)S(1)}, bf16[2,96,2,128]{3,1,2,0:T(8,128)(2,1)S(1)}, u32[]{:S(2)}, u32[]{:S(2)}) collective-permute-start(bf16[2,96,2,128]{3,1,2,0:T(8,128)(2,1)S(1)} %get-tuple-element.11), channel_id=1, source_target_pairs={{0,2},{2,0},{1,3},{3,1},{4,6},{6,4},{5,7},{7,5},{8,10},{10,8},{9,1... | collective-permute-start | bytes 294920 | tf_op jit(solution)/shard_map/ppermute | solution.py:14
  14.4 4.6 %collective-permute-start.3 = (bf16[2,96,2,128]{3,1,2,0:T(8,128)(2,1)S(1)}, bf16[2,96,2,128]{3,1,2,0:T(8,128)(2,1)S(1)}, u32[]{:S(2)}, u32[]{:S(2)}) collective-permute-start(bf16[2,96,2,128]{3,1,2,0:T(8,128)(2,1)S(1)} %get-tuple-element.12), channel_id=1, source_target_pairs={{2,0},{0,2},{3,1},{1,3},{6,4},{4,6},{7,5},{5,7},{10,8},{8,10},{11,... | collective-permute-start | bytes 294920 | tf_op jit(solution)/shard_map/ppermute | solution.py:17
  19.6 1.5 %collective-permute-start.4 = (bf16[2,96,12,2]{1,3,2,0:T(2,128)(2,1)S(1)}, bf16[2,96,12,2]{1,3,2,0:T(2,128)(2,1)S(1)}, u32[]{:S(2)}, u32[]{:S(2)}) collective-permute-start(bf16[2,96,12,2]{1,3,2,0:T(2,128)(2,1)S(1)} %copy.64), channel_id=1, source_target_pairs={{0,1},{1,0},{2,3},{3,2},{4,5},{5,4},{6,7},{7,6},{8,9},{9,8},{10,11... | collective-permute-start | bytes 27656 | tf_op jit(solution)/shard_map/ppermute | solution.py:14
  20.0 1.6 %collective-permute-start.5 = (bf16[2,96,12,2]{1,3,2,0:T(2,128)(2,1)S(1)}, bf16[2,96,12,2]{1,3,2,0:T(2,128)(2,1)S(1)}, u32[]{:S(2)}, u32[]{:S(2)}) collective-permute-start(bf16[2,96,12,2]{1,3,2,0:T(2,128)(2,1)S(1)} %copy.65), channel_id=1, source_target_pairs={{1,0},{0,1},{3,2},{2,3},{5,4},{4,5},{7,6},{6,7},{9,8},{8,9},{11,10... | collective-permute-start | bytes 27656 | tf_op jit(solution)/shard_map/ppermute | solution.py:17
  21.9 1.0 %copy-start.1 = (bf16[2,9,96,96]{3,2,1,0:T(8,128)(2,1)S(1)}, bf16[2,9,96,96]{3,2,1,0:T(8,128)(2,1)}, u32[]{:S(2)}) copy-start(bf16[2,9,96,96]{3,2,1,0:T(8,128)(2,1)} %param.14) | copy-start | bytes 995332
  32.7 0.8 %copy-start.2 = (f32[2,8,8,128]{3,2,1,0:T(8,128)S(1)}, f32[2,8,8,128]{3,2,1,0:T(8,128)}, u32[]{:S(2)}) copy-start(f32[2,8,8,128]{3,2,1,0:T(8,128)} %param.8) | copy-start | bytes 196612
  32.7 0.9 %copy-start.3 = (f32[2,8,8,128]{3,2,1,0:T(8,128)S(1)}, f32[2,8,8,128]{3,2,1,0:T(8,128)}, u32[]{:S(2)}) copy-start(f32[2,8,8,128]{3,2,1,0:T(8,128)} %param.10) | copy-start | bytes 196612
  32.7 0.9 %copy-start.4 = (f32[2,8,8,128]{3,2,1,0:T(8,128)S(1)}, f32[2,8,8,128]{3,2,1,0:T(8,128)}, u32[]{:S(2)}) copy-start(f32[2,8,8,128]{3,2,1,0:T(8,128)} %param.9) | copy-start | bytes 196612
  32.8 0.9 %copy-start.5 = (bf16[8,96]{1,0:T(8,128)(2,1)S(1)}, bf16[8,96]{1,0:T(8,128)(2,1)}, u32[]{:S(2)}) copy-start(bf16[8,96]{1,0:T(8,128)(2,1)} %param.15) | copy-start | bytes 4612
  34.8 5.5 %collective-permute-start.6 = (f32[2,8,8,128]{3,1,2,0:T(8,128)S(1)}, f32[2,8,8,128]{3,1,2,0:T(8,128)S(1)}, u32[]{:S(2)}, u32[]{:S(2)}) collective-permute-start(f32[2,8,8,128]{3,1,2,0:T(8,128)S(1)} %fusion.14), channel_id=1, source_target_pairs={{0,4},{4,8},{8,12},{1,5},{5,9},{9,13},{2,6},{6,10},{10,14},{3,7},{... | collective-permute-start | bytes 196616 | tf_op jit(solution)/shard_map/ppermute | solution.py:14
  38.5 6.2 %collective-permute-start.7 = (f32[2,8,8,128]{3,1,2,0:T(8,128)S(1)}, f32[2,8,8,128]{3,1,2,0:T(8,128)S(1)}, u32[]{:S(2)}, u32[]{:S(2)}) collective-permute-start(f32[2,8,8,128]{3,1,2,0:T(8,128)S(1)} %fusion.14), channel_id=1, source_target_pairs={{4,0},{8,4},{12,8},{5,1},{9,5},{13,9},{6,2},{10,6},{14,10},{7,3},{... | collective-permute-start | bytes 196616 | tf_op jit(solution)/shard_map/ppermute | solution.py:17
  45.5 4.7 %collective-permute-start.8 = (bf16[2,96,2,128]{3,1,2,0:T(8,128)(2,1)S(1)}, bf16[2,96,2,128]{3,1,2,0:T(8,128)(2,1)S(1)}, u32[]{:S(2)}, u32[]{:S(2)}) collective-permute-start(bf16[2,96,2,128]{3,1,2,0:T(8,128)(2,1)S(1)} %get-tuple-element.9), channel_id=1, source_target_pairs={{0,2},{2,0},{1,3},{3,1},{4,6},{6,4},{5,7},{7,5},{8,10},{10,8},{9,1... | collective-permute-start | bytes 294920 | tf_op jit(solution)/shard_map/ppermute | solution.py:14
  46.6 4.6 %collective-permute-start.9 = (bf16[2,96,2,128]{3,1,2,0:T(8,128)(2,1)S(1)}, bf16[2,96,2,128]{3,1,2,0:T(8,128)(2,1)S(1)}, u32[]{:S(2)}, u32[]{:S(2)}) collective-permute-start(bf16[2,96,2,128]{3,1,2,0:T(8,128)(2,1)S(1)} %get-tuple-element.10), channel_id=1, source_target_pairs={{2,0},{0,2},{3,1},{1,3},{6,4},{4,6},{7,5},{5,7},{10,8},{8,10},{11,... | collective-permute-start | bytes 294920 | tf_op jit(solution)/shard_map/ppermute | solution.py:17
  51.8 1.6 %collective-permute-start.10 = (bf16[2,96,12,2]{1,3,2,0:T(2,128)(2,1)S(1)}, bf16[2,96,12,2]{1,3,2,0:T(2,128)(2,1)S(1)}, u32[]{:S(2)}, u32[]{:S(2)}) collective-permute-start(bf16[2,96,12,2]{1,3,2,0:T(2,128)(2,1)S(1)} %copy.91), channel_id=1, source_target_pairs={{0,1},{1,0},{2,3},{3,2},{4,5},{5,4},{6,7},{7,6},{8,9},{9,8},{10,11... | collective-permute-start | bytes 27656 | tf_op jit(solution)/shard_map/ppermute | solution.py:14
  52.2 1.6 %collective-permute-start.11 = (bf16[2,96,12,2]{1,3,2,0:T(2,128)(2,1)S(1)}, bf16[2,96,12,2]{1,3,2,0:T(2,128)(2,1)S(1)}, u32[]{:S(2)}, u32[]{:S(2)}) collective-permute-start(bf16[2,96,12,2]{1,3,2,0:T(2,128)(2,1)S(1)} %copy.92), channel_id=1, source_target_pairs={{1,0},{0,1},{3,2},{2,3},{5,4},{4,5},{7,6},{6,7},{9,8},{8,9},{11,10... | collective-permute-start | bytes 27656 | tf_op jit(solution)/shard_map/ppermute | solution.py:17
where the time goes:
time: 67.4 us; the launch traced here: 66.9 us
  matrix products  24.1 us (36%)
  starting transfers between devices  16.6 us (25%)
  waiting for transfers between devices  14.3 us (21%)
  local copies, waits for them, and re-layouts  8.35 us (12%)
  other arithmetic  1.85 us (3%)
  between operations  1.72 us (3%)
    dot_general x34, matrix products, conv_valid(): jnp.einsum('oi,firw->forw', kernel[3 * row_off + col_off], part, preferre...  20.1 us
    ppermute x6, starting transfers between devices, extended_2(): lax.ppermute(lax.slice_in_dim(block, block.shape[dim] - width, None, axis...  11.4 us
    ppermute x6, waiting for transfers between devices, extended_2(): lax.ppermute(lax.slice_in_dim(block, 0, width, axis=dim), axis, backward)  8.56 us
    ppermute x6, waiting for transfers between devices, extended_2(): lax.ppermute(lax.slice_in_dim(block, block.shape[dim] - width, None, axis...  5.77 us
    ppermute x6, starting transfers between devices, extended_2(): lax.ppermute(lax.slice_in_dim(block, 0, width, axis=dim), axis, backward)  5.17 us
    unnamed x17, local copies, waits for them, and re-layouts  2.48 us
    dot_general x2, matrix products, score_all(): jnp.einsum('co,forw->fcrw', out_weight, merged, preferred_element_type=jn...  2.39 us
    mul x2, other arithmetic, rim_rows(): return values * inside.astype(values.dtype)[None, None, :, None]  1.67 us
  transfers between devices with their start and end apart: 12, of which 7 were waited for; matrix products, arithmetic and copies ran while one was open for 7% of the time, Pallas kernels for 0%

commit v1 on v0

v1 whole, which is shorter than its diff:
```python
import functools

import jax
import jax.numpy as jnp
from jax import lax
from jax.experimental import pallas as pl
from jax.experimental.pallas import tpu as pltpu
from jax.sharding import PartitionSpec as P

LANES = 128
REACH = 4
EDGE = 2 * REACH
BF = jnp.bfloat16
F32 = jnp.float32


def ring_edges(rows_of, rows, first, count, lanes):
    lane = lax.broadcasted_iota(jnp.int32, rows_of(0).shape, 1)
    tile = jnp.zeros(rows_of(0).shape, F32)
    for row in range(count):
        at = first + EDGE * row
        value = rows_of(rows + row)
        low = pltpu.roll(value, at % lanes, 1)
        high = pltpu.roll(value, (at + EDGE) % lanes, 1)
        tile = jnp.where((lane >= at) & (lane < at + REACH), low, tile)
        tile = jnp.where((lane >= at + REACH) & (lane < at + EDGE), high, tile)
    return tile


def pack_kernel(
    geometry, step_ref, prior, observed, weight, noise,
    state_out, base_out, lon_out, down_rows, down_edge, up_rows, up_edge, state, base,
):
    frames, chans, rows = geometry
    step = step_ref[0]
    spread = jnp.sqrt(jnp.full((chans, LANES), 2.0 * step, F32))
    for row in range(rows):
        for frame in range(frames):
            part = pl.ds(frame * chans * rows + row, chans, stride=rows)
            own = prior[part, :]
            state[row, frame * chans : (frame + 1) * chans, :] = own
            base[row, frame * chans : (frame + 1) * chans, :] = (
                own + step * (weight[part, :] * (observed[part, :] - own)) + spread * noise[part, :]
            )
    for row in range(rows):
        state_out[row] = state[row].astype(BF)
        base_out[row] = base[row]
    lon_out[0] = ring_edges(lambda r: state[r], 0, EDGE * REACH, rows, LANES).astype(BF)
    lon_out[1] = ring_edges(lambda r: base[r], 0, EDGE * 2, rows, LANES).astype(BF)
    for out, edge, start, at in (
        (down_rows, down_edge, rows - REACH, 0),
        (up_rows, up_edge, 0, rows + REACH),
    ):
        skip = start + 2 if at == 0 else start
        at_base = 0 if at == 0 else rows + 2
        for row in range(REACH):
            out[row] = state[start + row].astype(BF)
        for row in range(2):
            out[REACH + row] = base[skip + row].astype(BF)
        edge[0] = ring_edges(lambda r: state[r], start, EDGE * at, REACH, LANES).astype(BF)
        edge[1] = ring_edges(lambda r: base[r], skip, EDGE * at_base, 2, LANES).astype(BF)


def features(geometry, in_rows, own, prev, following, lift, act, halo):
    frames, ring = geometry
    dims = (((0,), (0,)), ((), ()))

    def lifted(tile):
        stacked = jnp.concatenate([prev[tile], own[tile], following[tile]], axis=0)
        turned = jnp.transpose(stacked.astype(F32)).astype(BF)
        return jnp.dot(turned, lift[0], preferred_element_type=F32) + jnp.dot(
            turned, lift[1], preferred_element_type=F32
        )

    halo[...] = lifted(in_rows)
    for row in range(in_rows):
        main = lifted(row)
        whole = jnp.concatenate([main, halo[row * EDGE : (row + 1) * EDGE, :]], axis=0)
        for frame in range(frames):
            store_shifts(act, frame, row, ring, whole[:, frame * LANES : (frame + 1) * LANES])


def store_shifts(act, frame, row, ring, value):
    act[0, frame, row, :ring, :] = pltpu.roll(value, 1, 0).astype(BF)
    act[1, frame, row, :ring, :] = value.astype(BF)
    act[2, frame, row, :ring, :] = pltpu.roll(value, ring - 1, 0).astype(BF)


def conv_pairs(act, frame, weight, first, count):
    pieces = [
        jnp.concatenate([act[col, frame, 2 * (first + p) + row] for p in range(count)], axis=0)
        for row in range(4)
        for col in range(3)
    ]
    return jnp.dot(jnp.concatenate(pieces, axis=1), weight[...], preferred_element_type=F32)


def gated(half):
    return half + half * jnp.tanh(half)


def convolve(geometry, in_rows, reach, act, act2, sums, conv_a, conv_b, top, bottom, emit):
    frames, ring, pad, chunk = geometry
    for frame in range(frames):
        pairs = (in_rows - 2) // 2
        for first in range(0, pairs, chunk):
            count = min(chunk, pairs - first)
            sums[: count * pad, :] = conv_pairs(act, frame, conv_a, first, count)
            for p in range(count):
                for q in range(2):
                    row = 1 + 2 * (first + p) + q
                    value = gated(sums[p * pad : p * pad + ring, q * LANES : (q + 1) * LANES])
                    if row < reach:
                        value = value * top
                    if row >= in_rows - reach:
                        value = value * bottom
                    store_shifts(act2, frame, row - 1, ring, value)
        pairs = (in_rows - 4) // 2
        for first in range(0, pairs, chunk):
            count = min(chunk, pairs - first)
            sums[: count * pad, :] = conv_pairs(act2, frame, conv_b, first, count)
            for p in range(count):
                for q in range(2):
                    row = 2 + 2 * (first + p) + q
                    value = gated(sums[p * pad : p * pad + ring, q * LANES : (q + 1) * LANES])
                    merged = act[1, frame, row, :ring, :].astype(F32) + value
                    emit(frame, row - 2, merged)


def edge_flags():
    lat = lax.axis_index("lat")
    top = jnp.where(lat > 0, 1.0, 0.0).astype(F32)
    bottom = jnp.where(lat < lax.axis_size("lat") - 1, 1.0, 0.0).astype(F32)
    return top, bottom


def project(out_weight, merged):
    return lax.dot_general(
        out_weight[...], merged, (((1,), (1,)), ((), ())), preferred_element_type=F32
    )


def first_kernel(
    geometry, step_ref, own, prev, following, base, base_edge, lift, conv_a, conv_b, out_weight,
    next_out, state_out, act, act2, sums, halo, halo_merged,
):
    frames, chans, rows, ring, pad, chunk = geometry
    in_rows, out_rows = rows + 2 * REACH, rows + 4
    top, bottom = edge_flags()
    step = step_ref[0]
    features((frames, ring), in_rows, own, prev, following, lift, act, halo)

    def emit(frame, row, merged):
        score = project(out_weight, merged[:LANES].astype(BF))
        part = slice(frame * chans, (frame + 1) * chans)
        if row < 2:
            start = base_edge[row, part, :].astype(F32)
        elif row < rows + 2:
            start = base[row - 2, part, :]
        else:
            start = base_edge[row - rows, part, :].astype(F32)
        value = start + step * score
        if row < 2:
            value = value * top
        if row >= rows + 2:
            value = value * bottom
        state_out[row, part, :] = value
        halo_merged[frame, row * EDGE : (row + 1) * EDGE, :] = merged[LANES:]

    convolve(
        (frames, ring, pad, chunk), in_rows, REACH, act, act2, sums, conv_a, conv_b, top, bottom, emit
    )
    for row in range(out_rows):
        next_out[row] = state_out[row].astype(BF)
    edges = [project(out_weight, halo_merged[frame].astype(BF)) for frame in range(frames)]
    score = jnp.concatenate(edges, axis=0)
    value = base_edge[4].astype(F32) + step * score
    lane = lax.broadcasted_iota(jnp.int32, value.shape, 1)
    value = jnp.where(lane < 2 * EDGE, value * top, value)
    value = jnp.where(lane >= (rows + 2) * EDGE, value * bottom, value)
    value = jnp.where(lane < out_rows * EDGE, value, 0.0)
    next_out[out_rows] = value.astype(BF)


def last_kernel(
    geometry, step_ref, own, prev, following, state, observed, weight, noise, lift, conv_a, conv_b,
    out_weight, result, act, act2, sums, halo,
):
    frames, chans, rows, ring, pad, chunk = geometry
    in_rows = rows + 4
    top, bottom = edge_flags()
    step = step_ref[1]
    spread = jnp.sqrt(jnp.full((chans, LANES), 2.0 * step, F32))
    features((frames, ring), in_rows, own, prev, following, lift, act, halo)

    def emit(frame, row, merged):
        score = project(out_weight, merged[:LANES].astype(BF))
        part = pl.ds(frame * chans * rows + row, chans, stride=rows)
        before = state[row + 2, frame * chans : (frame + 1) * chans, :]
        result[part, :] = (
            before
            + step * (score + weight[part, :] * (observed[part, :] - before))
            + spread * noise[part, :]
        )

    convolve((frames, ring, pad, chunk), in_rows, 2, act, act2, sums, conv_a, conv_b, top, bottom, emit)


def ring_perm(count, by):
    return [(i, (i + by) % count) for i in range(count)]


def lane_weights(lift_weight, conv_weights, out_weight):
    hidden, stacked = lift_weight.shape
    gap = LANES - hidden
    chans = out_weight.shape[0]
    turned = lift_weight.T
    lanes = [
        jnp.pad(turned, ((frame * chans, (1 - frame) * chans), (0, gap))) for frame in range(2)
    ]
    lift = jnp.concatenate(lanes, axis=1)
    block = 2 * chans
    tm = lax.axis_index("tm")
    kept = jnp.concatenate(
        [
            jnp.full((block, 1), jnp.where(tm > 0, 1.0, 0.0), F32),
            jnp.ones((block, 1), F32),
            jnp.full((block, 1), jnp.where(tm < lax.axis_size("tm") - 1, 1.0, 0.0), F32),
        ],
        axis=0,
    )
    lift = lift * kept
    high = lax.reduce_precision(lift, 8, 7)
    lift = jnp.stack([high.astype(BF), (lift - high).astype(BF)])
    half = conv_weights * jnp.asarray(0.5, BF)
    taps = jnp.swapaxes(half, 2, 3).reshape(2, 3, 3, hidden, hidden)
    taps = jnp.pad(taps, ((0, 0), (0, 0), (0, 0), (0, gap), (0, gap)))
    pair = jnp.concatenate(
        [
            jnp.pad(taps, ((0, 0), (0, 1), (0, 0), (0, 0), (0, 0))),
            jnp.pad(taps, ((0, 0), (1, 0), (0, 0), (0, 0), (0, 0))),
        ],
        axis=4,
    )
    conv = pair.reshape(2, 12 * LANES, 2 * LANES)
    return lift, conv[0], conv[1], jnp.pad(out_weight, ((0, 0), (0, gap)))


def per_device(
    prior_state, observed, obs_weight, noise_field, step_sizes, lift_weight, conv_weights, out_weight
):
    frames, chans, rows, cols = prior_state.shape
    lat_count, lon_count = lax.axis_size("lat"), lax.axis_size("lon")
    fc = frames * chans
    ring, pad, chunk = cols + EDGE, cols + 16, 4
    smem = pl.BlockSpec(memory_space=pltpu.SMEM)
    vmem = pl.BlockSpec(memory_space=pltpu.VMEM)
    shape = jax.ShapeDtypeStruct
    flat = lambda array: array.reshape(fc * rows, cols)

    packed = pl.pallas_call(
        functools.partial(pack_kernel, (frames, chans, rows)),
        out_shape=(
            shape((rows, fc, cols), BF),
            shape((rows, fc, cols), F32),
            shape((2, fc, cols), BF),
            shape((REACH + 2, fc, cols), BF),
            shape((2, fc, cols), BF),
            shape((REACH + 2, fc, cols), BF),
            shape((2, fc, cols), BF),
        ),
        in_specs=[smem] + [vmem] * 4,
        out_specs=[vmem] * 7,
        scratch_shapes=[pltpu.VMEM((rows, fc, cols), F32), pltpu.VMEM((rows, fc, cols), F32)],
    )(step_sizes, flat(prior_state), flat(observed), flat(obs_weight), flat(noise_field[0]))
    state, base, lon_edge, down_rows, down_edge, up_rows, up_edge = packed

    lat = lax.axis_index("lat")
    spot = ("lat", "lon")

    def lon_pick(array, axes, lat_shift):
        def move(by):
            perm = []
            for a in range(lat_count):
                for o in range(lon_count):
                    b = (a + lat_shift) % lat_count
                    perm.append((a * lon_count + o, b * lon_count + (o + by) % lon_count))
            return lax.ppermute(array, spot, perm)

        if lon_count <= 2:
            return move(lon_count - 1)
        lane = lax.broadcasted_iota(jnp.int32, array.shape, array.ndim - 1)
        return jnp.where(lane % EDGE < REACH, move(-1), move(1))

    has_top, has_bottom = lat > 0, lat < lat_count - 1
    side = lon_pick(lon_edge, spot, 0)
    if lat_count == 2:
        rows_in = lax.ppermute(jnp.where(has_top, up_rows, down_rows), "lat", ring_perm(2, 1))
        corner = lon_pick(jnp.where(has_top, up_edge, down_edge), spot, 1)
        from_top, from_bottom = rows_in, rows_in
        edge = side + corner
    else:
        from_top = lax.ppermute(down_rows, "lat", ring_perm(lat_count, 1))
        from_bottom = lax.ppermute(up_rows, "lat", ring_perm(lat_count, -1))
        zero = jnp.zeros_like(side)
        edge = (
            side
            + jnp.where(has_top, lon_pick(down_edge, spot, 1), zero)
            + jnp.where(has_bottom, lon_pick(up_edge, spot, -1), zero)
        )
    from_top = jnp.where(has_top, from_top, jnp.zeros_like(from_top))
    from_bottom = jnp.where(has_bottom, from_bottom, jnp.zeros_like(from_bottom))
    own = jnp.concatenate([from_top[:REACH], state, from_bottom[:REACH], edge[:1]], axis=0)
    base_edge = jnp.concatenate([from_top[REACH:], from_bottom[REACH:], edge[1:]], axis=0)

    lift, conv_a, conv_b, out_lanes = lane_weights(lift_weight, conv_weights, out_weight)
    tm_count = lax.axis_size("tm")

    def neighbours(array):
        return (
            lax.ppermute(array, "tm", ring_perm(tm_count, 1)),
            lax.ppermute(array, "tm", ring_perm(tm_count, -1)),
        )

    geometry = (frames, chans, rows, ring, pad, chunk)

    def scratch(in_rows):
        return [
            pltpu.VMEM((3, frames, in_rows, pad, LANES), BF),
            pltpu.VMEM((3, frames, in_rows - 2, pad, LANES), BF),
            pltpu.VMEM((chunk * pad, 2 * LANES), F32),
            pltpu.VMEM((LANES, 2 * LANES), F32),
        ]

    prev, following = neighbours(own)
    nxt, current = pl.pallas_call(
        functools.partial(first_kernel, geometry),
        out_shape=(shape((rows + 5, fc, cols), BF), shape((rows + 4, fc, cols), F32)),
        in_specs=[smem] + [vmem] * 9,
        out_specs=[vmem] * 2,
        scratch_shapes=scratch(rows + 2 * REACH) + [pltpu.VMEM((frames, LANES, LANES), F32)],
    )(step_sizes, own, prev, following, base, base_edge, lift, conv_a, conv_b, out_lanes)

    prev, following = neighbours(nxt)
    result = pl.pallas_call(
        functools.partial(last_kernel, geometry),
        out_shape=shape((fc * rows, cols), F32),
        in_specs=[smem] + [vmem] * 11,
        out_specs=vmem,
        scratch_shapes=scratch(rows + 4),
    )(
        step_sizes, nxt, prev, following, current, flat(observed), flat(obs_weight),
        flat(noise_field[1]), lift, conv_a, conv_b, out_lanes,
    )
    return result.reshape(prior_state.shape)


def solution(mesh):
    placed = (
        P(("groups", "tm"), None, "lat", "lon"),
        P(("groups", "tm"), None, "lat", "lon"),
        P(("groups", "tm"), None, "lat", "lon"),
        P(None, ("groups", "tm"), None, "lat", "lon"),
        P(),
        P(),
        P(),
        P(),
    )
    return jax.shard_map(
        per_device,
        mesh=mesh,
        in_specs=placed,
        out_specs=P(("groups", "tm"), None, "lat", "lon"),
        check_vma=False,
    )
```

time: 67.4 us -> 43.9 us (0.65)
  matrix products: 24.1 us -> 0 us
  Pallas kernels: 0 us -> 17.4 us
  waiting for transfers between devices: 14.3 us -> 4.73 us
  starting transfers between devices: 16.6 us -> 11.2 us
  local copies, waits for them, and re-layouts: 8.35 us -> 5.87 us
  other arithmetic: 1.85 us -> 4.14 us
  between operations: 1.72 us -> 0.12 us
    dot_general x38 -> x0, matrix products: 24.1 us -> none  [the longest x34 20.1 us: conv_valid(): jnp.einsum('oi,firw->forw', kernel[3 * row_off + col_off], part, preferre...]
    pallas_call x0 -> x3, Pallas kernels: none -> 17.4 us  [the longest x1 8.53 us: per_device(): pl.pallas_call(functools.partial(first_kernel, geometry), out_shape=(shap...]
    ppermute x12 -> x7, waiting for transfers between devices: 14.3 us -> 4.73 us  [the longest x2 4.24 us: neighbours(): lax.ppermute(array, 'tm', ring_perm(tm_count, 1))]
    ppermute x12 -> x7, starting transfers between devices: 16.6 us -> 11.2 us  [the longest x2 4.82 us: neighbours(): lax.ppermute(array, 'tm', ring_perm(tm_count, -1))]
    select_n x0 -> x3, other arithmetic: none -> 1.46 us  [the longest x1 0.74 us: per_device(): jnp.where(has_top, up_rows, down_rows)]
    ppermute x4 -> x0, local copies, waits for them, and re-layouts: 1.41 us -> none  [the longest x2 0.71 us: extended_2(): lax.ppermute(lax.slice_in_dim(block, block.shape[dim] - width, None, axis...]
    unnamed x17 -> x14, local copies, waits for them, and re-layouts: 2.48 us -> 1.27 us
    slice x10 -> x7, local copies, waits for them, and re-layouts: 3.8 us -> 2.81 us  [the longest x1 1.53 us: per_device(): noise_field[1]]
  transfers between devices with their start and end apart: 12 -> 7, of which waited for: 7 -> 3; matrix products, arithmetic and copies ran while one was open for 7% -> 15% of each run, Pallas kernels for 0% -> 0%
where the time goes in v1:
time: 43.9 us; the launch traced here: 43.4 us
  Pallas kernels  17.4 us (40%)
  starting transfers between devices  11.2 us (26%)
  local copies, waits for them, and re-layouts  5.87 us (13%)
  waiting for transfers between devices  4.73 us (11%)
  other arithmetic  4.14 us (9%)
    pallas_call x1, Pallas kernels, per_device(): pl.pallas_call(functools.partial(first_kernel, geometry), out_shape=(shap...  8.53 us
    pallas_call x1, Pallas kernels, per_device(): pl.pallas_call(functools.partial(last_kernel, geometry), out_shape=shape(...  7.15 us
    ppermute x2, starting transfers between devices, neighbours(): lax.ppermute(array, 'tm', ring_perm(tm_count, -1))  4.82 us
    ppermute x2, waiting for transfers between devices, neighbours(): lax.ppermute(array, 'tm', ring_perm(tm_count, 1))  4.24 us
    ppermute x2, starting transfers between devices, neighbours(): lax.ppermute(array, 'tm', ring_perm(tm_count, 1))  3.25 us
    ppermute x2, starting transfers between devices, move(): return lax.ppermute(array, spot, perm)  3.08 us
    pallas_call x1, Pallas kernels, per_device(): pl.pallas_call(functools.partial(pack_kernel, (frames, chans, rows)), out...  1.69 us
    slice x1, local copies, waits for them, and re-layouts, per_device(): noise_field[1]  1.53 us
  transfers between devices with their start and end apart: 7, of which 3 were waited for; matrix products, arithmetic and copies ran while one was open for 15% of the time, Pallas kernels for 0%

profile of v1, /device:TPU:0, one launch (start us, length us, event | category | flops | bytes accessed | tf_op | source)
XLA Modules:
  0.0 43.4 jit_solution(12280677273301300032)
XLA Ops:
  0.0 1.5 %fusion.6 = (f32[1,2,8,8,128]{4,3,2,1,0:T(8,128)}, f32[1,2,8,8,128]{4,3,2,1,0:T(8,128)}) fusion(f32[2,2,8,8,128]{4,3,2,1,0:T(8,128)} %param.11), kind=kLoop, calls=%fused_computation.23 | loop fusion | bytes 262144 | tf_op jit(solution)/shard_map/slice | solution.py:353
  1.5 1.7 %shard_map.82 = (bf16[8,16,128]{2,1,0:T(8,128)(2,1)}, f32[8,16,128]{2,1,0:T(8,128)}, bf16[2,16,128]{2,1,0:T(8,128)(2,1)}, bf16[6,16,128]{2,1,0:T(8,128)(2,1)}, b...) custom-call(f32[2]{0:T(128)} %step_ref.5, f32[128,128]{1,0:T(8,128)} %bitcast.39, ...), custom_call_target="tpu_custom_call" | custom-call | tf_op jit(solution)/shard_map/pallas_call | solution.py:261
  3.2 0.7 %broadcast_select_fusion.3 = bf16[2,16,128]{2,1,0:T(8,128)(2,1)S(1)} fusion(bf16[2,16,128]{2,1,0:T(8,128)(2,1)} %get-tuple-element.18, bf16[2,16,128]{2,1,0:T(8,128)(2,1)} %get-tuple-element.19, pred[]{:T(512)S(6)} %gt.6), kind=kLoop, calls=%fused_computation.18 | loop fusion | flops 4096 | bytes 24577 | tf_op jit(solution)/shard_map/jit(_where)/select_n | solution.py:299
  3.9 2.4 %collective-permute-start.2 = (bf16[2,16,128]{2,1,0:T(8,128)(2,1)S(1)}, bf16[2,16,128]{2,1,0:T(8,128)(2,1)S(1)}, u32[]{:S(2)}, u32[]{:S(2)}) collective-permute-start(bf16[2,16,128]{2,1,0:T(8,128)(2,1)S(1)} %broadcast_select_fusion.3), channel_id=1, source_target_pairs={{0,3},{1,2},{2,1},{3,0},{4,7},{5,6},{6,5},{7,4},{8,11},{9,10},{10,... | collective-permute-start | bytes 24584 | tf_op jit(solution)/shard_map/ppermute | solution.py:288
  6.3 0.7 %collective-permute-start.1 = (bf16[2,16,128]{2,1,0:T(8,128)(2,1)}, bf16[2,16,128]{2,1,0:T(8,128)(2,1)S(1)}, u32[]{:S(2)}, u32[]{:S(2)}) collective-permute-start(bf16[2,16,128]{2,1,0:T(8,128)(2,1)} %get-tuple-element.17), channel_id=1, source_target_pairs={{0,1},{1,0},{2,3},{3,2},{4,5},{5,4},{6,7},{7,6},{8,9},{9,8},{10,11... | collective-permute-start | bytes 24584 | tf_op jit(solution)/shard_map/ppermute | solution.py:288
  7.0 0.7 %broadcast_select_fusion.2 = bf16[6,16,128]{2,1,0:T(8,128)(2,1)S(1)} fusion(bf16[6,16,128]{2,1,0:T(8,128)(2,1)} %get-tuple-element.14, bf16[6,16,128]{2,1,0:T(8,128)(2,1)} %get-tuple-element.15, pred[]{:T(512)S(6)} %gt.6), kind=kLoop, calls=%fused_computation.16 | loop fusion | flops 12288 | bytes 73729 | tf_op jit(solution)/shard_map/jit(_where)/select_n | solution.py:298
  7.7 0.0 collective-permute-start
  7.8 0.8 %pad_bitcast_fusion.1 = (f32[1,48,128]{2,1,0:T(8,128)S(1)}, f32[1,48,128]{2,1,0:T(8,128)S(1)}) fusion(f32[40,96]{1,0:T(8,128)} %bitcast.40), kind=kLoop, calls=%fused_computation.13 | loop fusion | bytes 64512 | tf_op jit(solution)/shard_map/concatenate | solution.py:221
  8.6 1.1 %broadcast_multiply_fusion = bf16[2,9,96,96]{3,2,1,0:T(8,128)(2,1)S(1)} fusion(bf16[2,9,96,96]{3,2,1,0:T(8,128)(2,1)} %param.14), kind=kLoop, calls=%fused_computation.5 | loop fusion | flops 165888 | bytes 663552 | tf_op jit(solution)/shard_map/mul | solution.py:235
  9.6 0.3 copy.9
  9.9 0.2 pad.26
  10.0 0.2 fusion.2
  10.2 0.0 copy-start.6
  10.3 0.0 copy-start.5
  10.3 1.3 %fusion.5 = (bf16[1,4,3,128,256]{4,3,2,1,0:T(8,128)(2,1)}, bf16[1,4,3,128,256]{4,3,2,1,0:T(8,128)(2,1)}) fusion(bf16[2,4,3,128,256]{4,3,2,1,0:T(8,128)(2,1)S(1)} %fusion.2), kind=kLoop, calls=%fused_computation.22 | loop fusion | bytes 3145728 | tf_op jit(solution)/shard_map/slice | solution.py:246
  11.5 0.1 fusion.4
  11.6 0.1 reduce-precision_convert_fusion
  11.7 0.6 %pad_maximum_fusion.1.lift = bf16[2,48,256]{2,1,0:T(8,128)(2,1)} fusion(bf16[1,48,256]{2,1,0:T(8,128)(2,1)S(1)} %get-tuple-element.28, bf16[1,48,256]{2,1,0:T(8,128)(2,1)S(1)} %get-tuple-element.27), kind=kLoop, calls=%fused_computation.11 | loop fusion | flops 24576 | bytes 98304 | tf_op jit(solution)/shard_map/stack | solution.py:234
  12.3 0.0 copy-done.6
  12.3 0.6 %pad.29.out_weight = bf16[8,128]{1,0:T(8,128)(2,1)} pad(bf16[8,96]{1,0:T(8,128)(2,1)S(1)} %copy-done.6, bf16[]{:T(256)} %constant.8.clone.1), padding=0_0x0_32 | pad | bytes 3586 | tf_op jit(solution)/shard_map/jit(_pad)/pad | solution.py:246
  12.9 0.0 collective-permute-done.2
  12.9 0.0 collective-permute-done.1
  12.9 0.0 collective-permute-done
  13.0 0.0 copy-done.5
  13.0 0.0 copy-start
  13.0 2.2 %collective-permute-start.3 = (bf16[17,16,128]{2,1,0:T(8,128)(2,1)S(1)}, bf16[17,16,128]{2,1,0:T(8,128)(2,1)S(1)}, u32[]{:S(2)}, u32[]{:S(2)}) collective-permute-start(bf16[17,16,128]{2,1,0:T(8,128)(2,1)S(1)} %pad_maximum_fusion.own), channel_id=1, source_target_pairs={{0,4},{4,8},{8,12},{12,0},{1,5},{5,9},{9,13},{13,1},{2,6},{6,10},{... | collective-permute-start | bytes 208904 | tf_op jit(solution)/shard_map/ppermute | solution.py:321
  15.2 2.1 %collective-permute-start.4 = (bf16[17,16,128]{2,1,0:T(8,128)(2,1)S(1)}, bf16[17,16,128]{2,1,0:T(8,128)(2,1)S(1)}, u32[]{:S(2)}, u32[]{:S(2)}) collective-permute-start(bf16[17,16,128]{2,1,0:T(8,128)(2,1)S(1)} %pad_maximum_fusion.own), channel_id=1, source_target_pairs={{0,12},{4,0},{8,4},{12,8},{1,13},{5,1},{9,5},{13,9},{2,14},{6,2},{... | collective-permute-start | bytes 208904 | tf_op jit(solution)/shard_map/ppermute | solution.py:322
  17.3 0.6 %pad_maximum_fusion.2.base_edge = bf16[5,16,128]{2,1,0:T(8,128)(2,1)} fusion(bf16[1,16,128]{2,1,0:T(8,128)(2,1)S(1)} %get-tuple-element.33, bf16[2,16,128]{2,1,0:T(8,128)(2,1)S(1)} %slice.46, bf16[2,16,128]{2,1,0:T(8,128)(2,1)S(1)} %slice.45), kind=kLoop, calls=%fused_computation.17 | loop fusion | flops 20480 | bytes 40960 | tf_op jit(solution)/shard_map/concatenate | solution.py:314
  17.9 1.9 %collective-permute-done.3.prev = bf16[17,16,128]{2,1,0:T(8,128)(2,1)S(1)} collective-permute-done((bf16[17,16,128]{2,1,0:T(8,128)(2,1)S(1)}, bf16[17,16,128]{2,1,0:T(8,128)(2,1)S(1)}, u32[]{:S(2)}, u32[]{:S(2)}) %collective-permute-start.3) | collective-permute-done | bytes 69664 | tf_op jit(solution)/shard_map/ppermute | solution.py:321
  19.8 0.0 copy-start.1
  19.8 0.5 %collective-permute-done.4.following = bf16[17,16,128]{2,1,0:T(8,128)(2,1)S(1)} collective-permute-done((bf16[17,16,128]{2,1,0:T(8,128)(2,1)S(1)}, bf16[17,16,128]{2,1,0:T(8,128)(2,1)S(1)}, u32[]{:S(2)}, u32[]{:S(2)}) %collective-permute-start.4) | collective-permute-done | bytes 69664 | tf_op jit(solution)/shard_map/ppermute | solution.py:322
  20.2 0.0 copy-start.2
  20.2 0.0 copy-done
  20.2 0.1 copy-done.1
  20.4 0.5 %copy-done.2 = bf16[17,16,128]{2,1,0:T(8,128)(2,1)} copy-done((bf16[17,16,128]{2,1,0:T(8,128)(2,1)}, bf16[17,16,128]{2,1,0:T(8,128)(2,1)S(1)}, u32[]{:S(2)}) %copy-start.2) | copy-done | bytes 69656
  20.9 8.5 %shard_map.83 = (bf16[13,16,128]{2,1,0:T(8,128)(2,1)}, f32[12,16,128]{2,1,0:T(8,128)}) custom-call(f32[2]{0:T(128)} %step_ref.5, bf16[17,16,128]{2,1,0:T(8,128)(2,1)} %copy-done, bf16[17,16,128]{2,1,0:T(8,128)(2,1)} %copy-done.1, bf16[17,16,128]{2,1,0:T(8,128)(2,1)} %copy-done.2, f32[8,16,128]{2,1,0:T(8,128)} %get-tuple-element.20.base, ...), custom_call_target="tpu_custom_call" | custom-call | tf_op jit(solution)/shard_map/pallas_call | solution.py:336
  29.4 1.1 %collective-permute-start.5 = (bf16[13,16,128]{2,1,0:T(8,128)(2,1)}, bf16[13,16,128]{2,1,0:T(8,128)(2,1)S(1)}, u32[]{:S(2)}, u32[]{:S(2)}) collective-permute-start(bf16[13,16,128]{2,1,0:T(8,128)(2,1)} %get-tuple-element.21.own), channel_id=1, source_target_pairs={{0,4},{4,8},{8,12},{12,0},{1,5},{5,9},{9,13},{13,1},{2,6},{6,10},{... | collective-permute-start | bytes 159752 | tf_op jit(solution)/shard_map/ppermute | solution.py:321
  30.5 2.7 %collective-permute-start.6 = (bf16[13,16,128]{2,1,0:T(8,128)(2,1)}, bf16[13,16,128]{2,1,0:T(8,128)(2,1)S(1)}, u32[]{:S(2)}, u32[]{:S(2)}) collective-permute-start(bf16[13,16,128]{2,1,0:T(8,128)(2,1)} %get-tuple-element.21.own), channel_id=1, source_target_pairs={{0,12},{4,0},{8,4},{12,8},{1,13},{5,1},{9,5},{13,9},{2,14},{6,2},{... | collective-permute-start | bytes 159752 | tf_op jit(solution)/shard_map/ppermute | solution.py:322
  33.2 2.4 %collective-permute-done.5.prev = bf16[13,16,128]{2,1,0:T(8,128)(2,1)S(1)} collective-permute-done((bf16[13,16,128]{2,1,0:T(8,128)(2,1)}, bf16[13,16,128]{2,1,0:T(8,128)(2,1)S(1)}, u32[]{:S(2)}, u32[]{:S(2)}) %collective-permute-start.5) | collective-permute-done | bytes 53280 | tf_op jit(solution)/shard_map/ppermute | solution.py:321
  35.6 0.0 copy-start.3
  35.6 0.0 collective-permute-done.6.following
  35.6 0.0 copy-start.4
  35.6 0.6 %copy-done.3 = bf16[13,16,128]{2,1,0:T(8,128)(2,1)} copy-done((bf16[13,16,128]{2,1,0:T(8,128)(2,1)}, bf16[13,16,128]{2,1,0:T(8,128)(2,1)S(1)}, u32[]{:S(2)}) %copy-start.3) | copy-done | bytes 53272
  36.2 0.0 copy-done.4
  36.2 7.2 %shard_map.84 = f32[128,128]{1,0:T(8,128)} custom-call(f32[2]{0:T(128)} %step_ref.5, bf16[13,16,128]{2,1,0:T(8,128)(2,1)} %get-tuple-element.21.own, bf16[13,16,128]{2,1,0:T(8,128)(2,1)} %copy-done.3, bf16[13,16,128]{2,1,0:T(8,128)(2,1)} %copy-done.4, f32[12,16,128]{2,1,0:T(8,128)} %get-tuple-element.22.state, f32[128,128]{1,0:T(8,128)} %bitcast.34, ...), custom_call_target="tpu_custom_call" | custom-call | tf_op jit(solution)/shard_map/pallas_call | solution.py:345
  (11 shorter events, 0.0 us)
Async XLA Ops:
  3.9 9.0 %collective-permute-start.2 = (bf16[2,16,128]{2,1,0:T(8,128)(2,1)S(1)}, bf16[2,16,128]{2,1,0:T(8,128)(2,1)S(1)}, u32[]{:S(2)}, u32[]{:S(2)}) collective-permute-start(bf16[2,16,128]{2,1,0:T(8,128)(2,1)S(1)} %broadcast_select_fusion.3), channel_id=1, source_target_pairs={{0,3},{1,2},{2,1},{3,0},{4,7},{5,6},{6,5},{7,4},{8,11},{9,10},{10,... | collective-permute-start | bytes 24584 | tf_op jit(solution)/shard_map/ppermute | solution.py:288
  6.3 6.6 %collective-permute-start.1 = (bf16[2,16,128]{2,1,0:T(8,128)(2,1)}, bf16[2,16,128]{2,1,0:T(8,128)(2,1)S(1)}, u32[]{:S(2)}, u32[]{:S(2)}) collective-permute-start(bf16[2,16,128]{2,1,0:T(8,128)(2,1)} %get-tuple-element.17), channel_id=1, source_target_pairs={{0,1},{1,0},{2,3},{3,2},{4,5},{5,4},{6,7},{7,6},{8,9},{9,8},{10,11... | collective-permute-start | bytes 24584 | tf_op jit(solution)/shard_map/ppermute | solution.py:288
  7.7 5.2 %collective-permute-start = (bf16[6,16,128]{2,1,0:T(8,128)(2,1)S(1)}, bf16[6,16,128]{2,1,0:T(8,128)(2,1)S(1)}, u32[]{:S(2)}, u32[]{:S(2)}) collective-permute-start(bf16[6,16,128]{2,1,0:T(8,128)(2,1)S(1)} %broadcast_select_fusion.2), channel_id=1, source_target_pairs={{0,2},{2,0},{1,3},{3,1},{4,6},{6,4},{5,7},{7,5},{8,10},{10,8},{9,1... | collective-permute-start | bytes 73736 | tf_op jit(solution)/shard_map/ppermute | solution.py:298
  10.2 2.1 %copy-start.6 = (bf16[8,96]{1,0:T(8,128)(2,1)S(1)}, bf16[8,96]{1,0:T(8,128)(2,1)}, u32[]{:S(2)}) copy-start(bf16[8,96]{1,0:T(8,128)(2,1)} %param.15) | copy-start | bytes 4612
  10.3 2.7 %copy-start.5 = (bf16[8,16,128]{2,1,0:T(8,128)(2,1)S(1)}, bf16[8,16,128]{2,1,0:T(8,128)(2,1)}, u32[]{:S(2)}) copy-start(bf16[8,16,128]{2,1,0:T(8,128)(2,1)} %get-tuple-element.16) | copy-start | bytes 98308
  13.0 7.2 %copy-start = (bf16[17,16,128]{2,1,0:T(8,128)(2,1)}, bf16[17,16,128]{2,1,0:T(8,128)(2,1)S(1)}, u32[]{:S(2)}) copy-start(bf16[17,16,128]{2,1,0:T(8,128)(2,1)S(1)} %pad_maximum_fusion.own) | copy-start | bytes 208900
  13.0 6.7 %collective-permute-start.3 = (bf16[17,16,128]{2,1,0:T(8,128)(2,1)S(1)}, bf16[17,16,128]{2,1,0:T(8,128)(2,1)S(1)}, u32[]{:S(2)}, u32[]{:S(2)}) collective-permute-start(bf16[17,16,128]{2,1,0:T(8,128)(2,1)S(1)} %pad_maximum_fusion.own), channel_id=1, source_target_pairs={{0,4},{4,8},{8,12},{12,0},{1,5},{5,9},{9,13},{13,1},{2,6},{6,10},{... | collective-permute-start | bytes 208904 | tf_op jit(solution)/shard_map/ppermute | solution.py:321
  15.2 5.1 %collective-permute-start.4 = (bf16[17,16,128]{2,1,0:T(8,128)(2,1)S(1)}, bf16[17,16,128]{2,1,0:T(8,128)(2,1)S(1)}, u32[]{:S(2)}, u32[]{:S(2)}) collective-permute-start(bf16[17,16,128]{2,1,0:T(8,128)(2,1)S(1)} %pad_maximum_fusion.own), channel_id=1, source_target_pairs={{0,12},{4,0},{8,4},{12,8},{1,13},{5,1},{9,5},{13,9},{2,14},{6,2},{... | collective-permute-start | bytes 208904 | tf_op jit(solution)/shard_map/ppermute | solution.py:322
  19.8 0.6 %copy-start.1 = (bf16[17,16,128]{2,1,0:T(8,128)(2,1)}, bf16[17,16,128]{2,1,0:T(8,128)(2,1)S(1)}, u32[]{:S(2)}) copy-start(bf16[17,16,128]{2,1,0:T(8,128)(2,1)S(1)} %collective-permute-done.3.prev) | copy-start | bytes 208900
  20.2 0.6 %copy-start.2 = (bf16[17,16,128]{2,1,0:T(8,128)(2,1)}, bf16[17,16,128]{2,1,0:T(8,128)(2,1)S(1)}, u32[]{:S(2)}) copy-start(bf16[17,16,128]{2,1,0:T(8,128)(2,1)S(1)} %collective-permute-done.4.following) | copy-start | bytes 208900
  29.4 6.2 %collective-permute-start.5 = (bf16[13,16,128]{2,1,0:T(8,128)(2,1)}, bf16[13,16,128]{2,1,0:T(8,128)(2,1)S(1)}, u32[]{:S(2)}, u32[]{:S(2)}) collective-permute-start(bf16[13,16,128]{2,1,0:T(8,128)(2,1)} %get-tuple-element.21.own), channel_id=1, source_target_pairs={{0,4},{4,8},{8,12},{12,0},{1,5},{5,9},{9,13},{13,1},{2,6},{6,10},{... | collective-permute-start | bytes 159752 | tf_op jit(solution)/shard_map/ppermute | solution.py:321
  30.5 5.1 %collective-permute-start.6 = (bf16[13,16,128]{2,1,0:T(8,128)(2,1)}, bf16[13,16,128]{2,1,0:T(8,128)(2,1)S(1)}, u32[]{:S(2)}, u32[]{:S(2)}) collective-permute-start(bf16[13,16,128]{2,1,0:T(8,128)(2,1)} %get-tuple-element.21.own), channel_id=1, source_target_pairs={{0,12},{4,0},{8,4},{12,8},{1,13},{5,1},{9,5},{13,9},{2,14},{6,2},{... | collective-permute-start | bytes 159752 | tf_op jit(solution)/shard_map/ppermute | solution.py:322
  35.6 0.6 %copy-start.3 = (bf16[13,16,128]{2,1,0:T(8,128)(2,1)}, bf16[13,16,128]{2,1,0:T(8,128)(2,1)S(1)}, u32[]{:S(2)}) copy-start(bf16[13,16,128]{2,1,0:T(8,128)(2,1)S(1)} %collective-permute-done.5.prev) | copy-start | bytes 159748
  35.6 0.6 %copy-start.4 = (bf16[13,16,128]{2,1,0:T(8,128)(2,1)}, bf16[13,16,128]{2,1,0:T(8,128)(2,1)S(1)}, u32[]{:S(2)}) copy-start(bf16[13,16,128]{2,1,0:T(8,128)(2,1)S(1)} %collective-permute-done.6.following) | copy-start | bytes 159748

commit v2 on v1

--- a/solution.py
+++ b/solution.py
@@ -10,6 +10,7 @@
 LANES = 128
 REACH = 4
 EDGE = 2 * REACH
+GRANT = 24 << 20
 BF = jnp.bfloat16
 F32 = jnp.float32
 
@@ -29,9 +30,10 @@
 
 def pack_kernel(
     geometry, step_ref, prior, observed, weight, noise,
-    state_out, base_out, lon_out, down_rows, down_edge, up_rows, up_edge, state, base,
+    state_out, base_out, lon_out, *rest,
 ):
-    frames, chans, rows = geometry
+    frames, chans, rows, single = geometry
+    *outs, state, base = rest
     step = step_ref[0]
     spread = jnp.sqrt(jnp.full((chans, LANES), 2.0 * step, F32))
     for row in range(rows):
@@ -47,18 +49,22 @@
         base_out[row] = base[row]
     lon_out[0] = ring_edges(lambda r: state[r], 0, EDGE * REACH, rows, LANES).astype(BF)
     lon_out[1] = ring_edges(lambda r: base[r], 0, EDGE * 2, rows, LANES).astype(BF)
-    for out, edge, start, at in (
-        (down_rows, down_edge, rows - REACH, 0),
-        (up_rows, up_edge, 0, rows + REACH),
-    ):
+    sides = []
+    for start, at in ((rows - REACH, 0), (0, rows + REACH)):
         skip = start + 2 if at == 0 else start
         at_base = 0 if at == 0 else rows + 2
-        for row in range(REACH):
-            out[row] = state[start + row].astype(BF)
-        for row in range(2):
-            out[REACH + row] = base[skip + row].astype(BF)
-        edge[0] = ring_edges(lambda r: state[r], start, EDGE * at, REACH, LANES).astype(BF)
-        edge[1] = ring_edges(lambda r: base[r], skip, EDGE * at_base, 2, LANES).astype(BF)
+        tiles = [state[start + row] for row in range(REACH)] + [base[skip + row] for row in range(2)]
+        tiles.append(ring_edges(lambda r: state[r], start, EDGE * at, REACH, LANES))
+        tiles.append(ring_edges(lambda r: base[r], skip, EDGE * at_base, 2, LANES))
+        sides.append(tiles)
+    if single:
+        upward = lax.axis_index("lat") > 0
+        sides = [[jnp.where(upward, up, down) for down, up in zip(*sides)]]
+    for tiles, rows_out, edge_out in zip(sides, outs[::2], outs[1::2]):
+        for place, tile in enumerate(tiles[: REACH + 2]):
+            rows_out[place] = tile.astype(BF)
+        for place, tile in enumerate(tiles[REACH + 2 :]):
+            edge_out[place] = tile.astype(BF)
 
 
 def features(geometry, in_rows, own, prev, following, lift, act, halo):
@@ -196,11 +202,12 @@
     def emit(frame, row, merged):
         score = project(out_weight, merged[:LANES].astype(BF))
         part = pl.ds(frame * chans * rows + row, chans, stride=rows)
+        late = pl.ds((frames + frame) * chans * rows + row, chans, stride=rows)
         before = state[row + 2, frame * chans : (frame + 1) * chans, :]
         result[part, :] = (
             before
             + step * (score + weight[part, :] * (observed[part, :] - before))
-            + spread * noise[part, :]
+            + spread * noise[late, :]
         )
 
     convolve((frames, ring, pad, chunk), in_rows, 2, act, act2, sums, conv_a, conv_b, top, bottom, emit)
@@ -258,22 +265,22 @@
     shape = jax.ShapeDtypeStruct
     flat = lambda array: array.reshape(fc * rows, cols)
 
-    packed = pl.pallas_call(
-        functools.partial(pack_kernel, (frames, chans, rows)),
+    sides = (shape((REACH + 2, fc, cols), BF), shape((2, fc, cols), BF)) * (
+        1 if lat_count == 2 else 2
+    )
+    state, base, lon_edge, *outward = pl.pallas_call(
+        functools.partial(pack_kernel, (frames, chans, rows, lat_count == 2)),
         out_shape=(
             shape((rows, fc, cols), BF),
             shape((rows, fc, cols), F32),
             shape((2, fc, cols), BF),
-            shape((REACH + 2, fc, cols), BF),
-            shape((2, fc, cols), BF),
-            shape((REACH + 2, fc, cols), BF),
-            shape((2, fc, cols), BF),
+            *sides,
         ),
         in_specs=[smem] + [vmem] * 4,
-        out_specs=[vmem] * 7,
+        out_specs=[vmem] * (3 + len(sides)),
         scratch_shapes=[pltpu.VMEM((rows, fc, cols), F32), pltpu.VMEM((rows, fc, cols), F32)],
-    )(step_sizes, flat(prior_state), flat(observed), flat(obs_weight), flat(noise_field[0]))
-    state, base, lon_edge, down_rows, down_edge, up_rows, up_edge = packed
+        compiler_params=pltpu.CompilerParams(vmem_limit_bytes=GRANT),
+    )(step_sizes, flat(prior_state), flat(observed), flat(obs_weight), noise_field.reshape(-1, cols))
 
     lat = lax.axis_index("lat")
     spot = ("lat", "lon")
@@ -295,11 +302,12 @@
     has_top, has_bottom = lat > 0, lat < lat_count - 1
     side = lon_pick(lon_edge, spot, 0)
     if lat_count == 2:
-        rows_in = lax.ppermute(jnp.where(has_top, up_rows, down_rows), "lat", ring_perm(2, 1))
-        corner = lon_pick(jnp.where(has_top, up_edge, down_edge), spot, 1)
+        rows_in = lax.ppermute(outward[0], "lat", ring_perm(2, 1))
+        corner = lon_pick(outward[1], spot, 1)
         from_top, from_bottom = rows_in, rows_in
         edge = side + corner
     else:
+        down_rows, down_edge, up_rows, up_edge = outward
         from_top = lax.ppermute(down_rows, "lat", ring_perm(lat_count, 1))
         from_bottom = lax.ppermute(up_rows, "lat", ring_perm(lat_count, -1))
         zero = jnp.zeros_like(side)
@@ -339,6 +347,7 @@
         in_specs=[smem] + [vmem] * 9,
         out_specs=[vmem] * 2,
         scratch_shapes=scratch(rows + 2 * REACH) + [pltpu.VMEM((frames, LANES, LANES), F32)],
+        compiler_params=pltpu.CompilerParams(vmem_limit_bytes=GRANT),
     )(step_sizes, own, prev, following, base, base_edge, lift, conv_a, conv_b, out_lanes)
 
     prev, following = neighbours(nxt)
@@ -348,9 +357,10 @@
         in_specs=[smem] + [vmem] * 11,
         out_specs=vmem,
         scratch_shapes=scratch(rows + 4),
+        compiler_params=pltpu.CompilerParams(vmem_limit_bytes=GRANT),
     )(
         step_sizes, nxt, prev, following, current, flat(observed), flat(obs_weight),
-        flat(noise_field[1]), lift, conv_a, conv_b, out_lanes,
+        noise_field.reshape(-1, cols), lift, conv_a, conv_b, out_lanes,
     )
     return result.reshape(prior_state.shape)
 

time: 43.9 us -> 37.9 us (0.86)
  Pallas kernels: 17.4 us -> 13.7 us
  other arithmetic: 4.14 us -> 1.47 us
  waiting for transfers between devices: 4.73 us -> 5.53 us
    unnamed x14 -> x20, local copies, waits for them, and re-layouts: 1.27 us -> 4.36 us
    pallas_call x1, Pallas kernels: 8.53 us -> 6.88 us  [per_device(): pl.pallas_call(functools.partial(first_kernel, geometry), out_shape=(shap...]
    slice x1 -> x0, local copies, waits for them, and re-layouts: 1.53 us -> none  [per_device(): noise_field[1]]
    select_n x2 -> x0, other arithmetic: 1.45 us -> none  [the longest x1 0.74 us: per_device(): jnp.where(has_top, up_rows, down_rows)]
    slice x1, local copies, waits for them, and re-layouts: 1.27 us -> 0.14 us  [lane_weights(): return (lift, conv[0], conv[1], jnp.pad(out_weight, ((0, 0), (0, gap))))]
    pallas_call x1, Pallas kernels: 7.15 us -> 6.1 us  [per_device(): pl.pallas_call(functools.partial(last_kernel, geometry), out_shape=shape(...]
    pallas_call x1, Pallas kernels: 1.69 us -> 0.68 us  [per_device(): pl.pallas_call(functools.partial(pack_kernel, (frames, chans, rows, lat_c...]
    ppermute x2, waiting for transfers between devices: 4.24 us -> 4.88 us  [neighbours(): lax.ppermute(array, 'tm', ring_perm(tm_count, 1))]
  transfers between devices with their start and end apart: 7 -> 7, of which waited for: 3 -> 4; matrix products, arithmetic and copies ran while one was open for 15% -> 8% of each run, Pallas kernels for 0% -> 0%
where the time goes in v2:
time: 37.9 us; the launch traced here: 37.5 us
  Pallas kernels  13.7 us (36%)
  starting transfers between devices  10.9 us (29%)
  local copies, waits for them, and re-layouts  5.75 us (15%)
  waiting for transfers between devices  5.53 us (15%)
  other arithmetic  1.47 us (4%)
    pallas_call x1, Pallas kernels, per_device(): pl.pallas_call(functools.partial(first_kernel, geometry), out_shape=(shap...  6.88 us
    pallas_call x1, Pallas kernels, per_device(): pl.pallas_call(functools.partial(last_kernel, geometry), out_shape=shape(...  6.1 us
    ppermute x2, starting transfers between devices, neighbours(): lax.ppermute(array, 'tm', ring_perm(tm_count, -1))  4.95 us
    ppermute x2, waiting for transfers between devices, neighbours(): lax.ppermute(array, 'tm', ring_perm(tm_count, 1))  4.88 us
    unnamed x20, local copies, waits for them, and re-layouts  4.36 us
    ppermute x2, starting transfers between devices, move(): return lax.ppermute(array, spot, perm)  3.15 us
    ppermute x2, starting transfers between devices, neighbours(): lax.ppermute(array, 'tm', ring_perm(tm_count, 1))  2.81 us
    mul x1, other arithmetic, lane_weights(): half = conv_weights * jnp.asarray(0.5, BF)  1.05 us
  transfers between devices with their start and end apart: 7, of which 4 were waited for; matrix products, arithmetic and copies ran while one was open for 8% of the time, Pallas kernels for 0%

profile of v2, /device:TPU:0, one launch (start us, length us, event | category | flops | bytes accessed | tf_op | source)
XLA Modules:
  0.0 37.5 jit_solution(4926912296431687719)
XLA Ops:
  0.0 0.0 copy-start
  0.0 0.9 %copy-done = f32[2,2,8,8,128]{4,3,2,1,0:T(8,128)S(1)} copy-done((f32[2,2,8,8,128]{4,3,2,1,0:T(8,128)S(1)}, f32[2,2,8,8,128]{4,3,2,1,0:T(8,128)}, u32[]{:S(2)}) %copy-start) | copy-done | bytes 131096
  0.9 0.0 copy-start.2
  0.9 0.8 %copy-done.2 = f32[2,8,8,128]{3,2,1,0:T(8,128)S(1)} copy-done((f32[2,8,8,128]{3,2,1,0:T(8,128)S(1)}, f32[2,8,8,128]{3,2,1,0:T(8,128)}, u32[]{:S(2)}) %copy-start.2) | copy-done | bytes 65560
  1.7 0.0 copy-start.4
  1.7 0.8 %copy-done.4 = f32[2,8,8,128]{3,2,1,0:T(8,128)S(1)} copy-done((f32[2,8,8,128]{3,2,1,0:T(8,128)S(1)}, f32[2,8,8,128]{3,2,1,0:T(8,128)}, u32[]{:S(2)}) %copy-start.4) | copy-done | bytes 65560
  2.6 0.0 copy-start.6
  2.6 0.8 %copy-done.6 = f32[2,8,8,128]{3,2,1,0:T(8,128)S(1)} copy-done((f32[2,8,8,128]{3,2,1,0:T(8,128)S(1)}, f32[2,8,8,128]{3,2,1,0:T(8,128)}, u32[]{:S(2)}) %copy-start.6) | copy-done | bytes 65560
  3.4 0.0 copy-start.7
  3.4 0.7 %copy-done.7 = f32[2]{0:T(128)S(1)} copy-done((f32[2]{0:T(128)S(1)}, f32[2]{0:T(128)}, u32[]{:S(2)}) %copy-start.7) | copy-done | bytes 32
  4.1 0.7 %shard_map.82 = (bf16[8,16,128]{2,1,0:T(8,128)(2,1)S(1)}, f32[8,16,128]{2,1,0:T(8,128)S(1)}, bf16[2,16,128]{2,1,0:T(8,128)(2,1)S(1)}, bf16[6,16,128]{2,1,0:T(8,128)(2,1)S(1)}, bf16[2,16,128]{2,1,0:T(8,128)(2,1)S(1)}) custom-call(f32[2]{0:T(128)S(1)} %copy-done.7, f32[128,128]{1,0:T(8,128)S(1)} %bitcast.37, f32[128,128]{1,0:T(8,128)S(1)} %bitcast.33, ...), custom_call_target="tpu_custom_call" | custom-call | tf_op jit(solution)/shard_map/pallas_call | solution.py:271
  4.8 0.6 %collective-permute-start.1 = (bf16[2,16,128]{2,1,0:T(8,128)(2,1)S(1)}, bf16[2,16,128]{2,1,0:T(8,128)(2,1)S(1)}, u32[]{:S(2)}, u32[]{:S(2)}) collective-permute-start(bf16[2,16,128]{2,1,0:T(8,128)(2,1)S(1)} %get-tuple-element.14), channel_id=1, source_target_pairs={{0,1},{1,0},{2,3},{3,2},{4,5},{5,4},{6,7},{7,6},{8,9},{9,8},{10,11... | collective-permute-start | bytes 24584 | tf_op jit(solution)/shard_map/ppermute | solution.py:295
  5.3 2.6 %collective-permute-start.2 = (bf16[2,16,128]{2,1,0:T(8,128)(2,1)S(1)}, bf16[2,16,128]{2,1,0:T(8,128)(2,1)S(1)}, u32[]{:S(2)}, u32[]{:S(2)}) collective-permute-start(bf16[2,16,128]{2,1,0:T(8,128)(2,1)S(1)} %get-tuple-element.15), channel_id=1, source_target_pairs={{0,3},{1,2},{2,1},{3,0},{4,7},{5,6},{6,5},{7,4},{8,11},{9,10},{10,... | collective-permute-start | bytes 24584 | tf_op jit(solution)/shard_map/ppermute | solution.py:295
  7.9 0.0 collective-permute-start
  8.0 0.8 %pad_bitcast_fusion.1 = (f32[1,48,128]{2,1,0:T(8,128)S(1)}, f32[1,48,128]{2,1,0:T(8,128)S(1)}) fusion(f32[40,96]{1,0:T(8,128)} %bitcast.39), kind=kLoop, calls=%fused_computation.13 | loop fusion | bytes 64512 | tf_op jit(solution)/shard_map/concatenate | solution.py:228
  8.8 1.1 %broadcast_multiply_fusion = bf16[2,9,96,96]{3,2,1,0:T(8,128)(2,1)S(1)} fusion(bf16[2,9,96,96]{3,2,1,0:T(8,128)(2,1)} %param.14), kind=kLoop, calls=%fused_computation.5 | loop fusion | flops 165888 | bytes 663552 | tf_op jit(solution)/shard_map/mul | solution.py:242
  9.8 0.3 copy.9
  10.1 0.2 pad.26
  10.2 0.2 fusion.2
  10.5 0.0 copy-start.9
  10.5 0.0 copy-start.8
  10.5 0.1 fusion.5
  10.6 0.0 copy-start.1
  10.6 0.0 copy-start.3
  10.7 0.0 copy-start.5
  10.7 0.1 fusion.4
  10.8 0.1 reduce-precision_convert_fusion
  10.9 0.3 copy-done.9
  11.1 0.0 collective-permute-done.1
  11.2 0.0 collective-permute-done.2
  11.2 0.6 %collective-permute-done = bf16[6,16,128]{2,1,0:T(8,128)(2,1)S(1)} collective-permute-done((bf16[6,16,128]{2,1,0:T(8,128)(2,1)S(1)}, bf16[6,16,128]{2,1,0:T(8,128)(2,1)S(1)}, u32[]{:S(2)}, u32[]{:S(2)}) %collective-permute-start) | collective-permute-done | bytes 24608 | tf_op jit(solution)/shard_map/ppermute | solution.py:305
  11.8 1.6 %collective-permute-start.3 = (bf16[17,16,128]{2,1,0:T(8,128)(2,1)S(1)}, bf16[17,16,128]{2,1,0:T(8,128)(2,1)S(1)}, u32[]{:S(2)}, u32[]{:S(2)}) collective-permute-start(bf16[17,16,128]{2,1,0:T(8,128)(2,1)S(1)} %pad_maximum_fusion.own), channel_id=1, source_target_pairs={{0,4},{4,8},{8,12},{12,0},{1,5},{5,9},{9,13},{13,1},{2,6},{6,10},{... | collective-permute-start | bytes 208904 | tf_op jit(solution)/shard_map/ppermute | solution.py:329
  13.4 2.2 %collective-permute-start.4 = (bf16[17,16,128]{2,1,0:T(8,128)(2,1)S(1)}, bf16[17,16,128]{2,1,0:T(8,128)(2,1)S(1)}, u32[]{:S(2)}, u32[]{:S(2)}) collective-permute-start(bf16[17,16,128]{2,1,0:T(8,128)(2,1)S(1)} %pad_maximum_fusion.own), channel_id=1, source_target_pairs={{0,12},{4,0},{8,4},{12,8},{1,13},{5,1},{9,5},{13,9},{2,14},{6,2},{... | collective-permute-start | bytes 208904 | tf_op jit(solution)/shard_map/ppermute | solution.py:330
  15.7 2.7 %collective-permute-done.3.prev = bf16[17,16,128]{2,1,0:T(8,128)(2,1)S(1)} collective-permute-done((bf16[17,16,128]{2,1,0:T(8,128)(2,1)S(1)}, bf16[17,16,128]{2,1,0:T(8,128)(2,1)S(1)}, u32[]{:S(2)}, u32[]{:S(2)}) %collective-permute-start.3) | collective-permute-done | bytes 69664 | tf_op jit(solution)/shard_map/ppermute | solution.py:329
  18.4 0.1 collective-permute-done.4.following
  18.5 0.0 copy-done.8
  18.5 6.9 %shard_map.83 = (bf16[13,16,128]{2,1,0:T(8,128)(2,1)S(1)}, f32[12,16,128]{2,1,0:T(8,128)S(1)}) custom-call(f32[2]{0:T(128)S(1)} %copy-done.8, bf16[17,16,128]{2,1,0:T(8,128)(2,1)S(1)} %pad_maximum_fusion.own, bf16[17,16,128]{2,1,0:T(8,128)(2,1)S(1)} %collective-permute-done.3.prev, bf16[17,16,128]{2,1,0:T(8,128)(2,1)S(1)} %collective-permute-done.4.following, ...), custom_call_target="tpu_custom_call" | custom-call | tf_op jit(solution)/shard_map/pallas_call | solution.py:344
  25.4 1.2 %collective-permute-start.5 = (bf16[13,16,128]{2,1,0:T(8,128)(2,1)S(1)}, bf16[13,16,128]{2,1,0:T(8,128)(2,1)S(1)}, u32[]{:S(2)}, u32[]{:S(2)}) collective-permute-start(bf16[13,16,128]{2,1,0:T(8,128)(2,1)S(1)} %get-tuple-element.17.own), channel_id=1, source_target_pairs={{0,4},{4,8},{8,12},{12,0},{1,5},{5,9},{9,13},{13,1},{2,6},{6,10},{... | collective-permute-start | bytes 159752 | tf_op jit(solution)/shard_map/ppermute | solution.py:329
  26.5 2.7 %collective-permute-start.6 = (bf16[13,16,128]{2,1,0:T(8,128)(2,1)S(1)}, bf16[13,16,128]{2,1,0:T(8,128)(2,1)S(1)}, u32[]{:S(2)}, u32[]{:S(2)}) collective-permute-start(bf16[13,16,128]{2,1,0:T(8,128)(2,1)S(1)} %get-tuple-element.17.own), channel_id=1, source_target_pairs={{0,12},{4,0},{8,4},{12,8},{1,13},{5,1},{9,5},{13,9},{2,14},{6,2},{... | collective-permute-start | bytes 159752 | tf_op jit(solution)/shard_map/ppermute | solution.py:330
  29.2 2.2 %collective-permute-done.5.prev = bf16[13,16,128]{2,1,0:T(8,128)(2,1)S(1)} collective-permute-done((bf16[13,16,128]{2,1,0:T(8,128)(2,1)S(1)}, bf16[13,16,128]{2,1,0:T(8,128)(2,1)S(1)}, u32[]{:S(2)}, u32[]{:S(2)}) %collective-permute-start.5) | collective-permute-done | bytes 53280 | tf_op jit(solution)/shard_map/ppermute | solution.py:329
  31.4 0.0 collective-permute-done.6.following
  31.4 0.0 copy-done.1
  31.4 0.0 copy-done.3
  31.4 0.0 copy-done.5
  31.4 6.1 %shard_map.84 = f32[128,128]{1,0:T(8,128)} custom-call(f32[2]{0:T(128)S(1)} %copy-done.8, bf16[13,16,128]{2,1,0:T(8,128)(2,1)S(1)} %get-tuple-element.17.own, bf16[13,16,128]{2,1,0:T(8,128)(2,1)S(1)} %collective-permute-done.5.prev, bf16[13,16,128]{2,1,0:T(8,128)(2,1)S(1)} %collective-permute-done.6.following, f32[12,16,128]{2,1,0:T(8,128)S(1)} %get-tuple-element.18.state, ...), custom_call_target="tpu_custom_call" | custom-call | tf_op jit(solution)/shard_map/pallas_call | solution.py:354
  (14 shorter events, 0.1 us)
Async XLA Ops:
  0.0 0.9 %copy-start = (f32[2,2,8,8,128]{4,3,2,1,0:T(8,128)S(1)}, f32[2,2,8,8,128]{4,3,2,1,0:T(8,128)}, u32[]{:S(2)}) copy-start(f32[2,2,8,8,128]{4,3,2,1,0:T(8,128)} %param.11) | copy-start | bytes 393220
  0.9 0.8 %copy-start.2 = (f32[2,8,8,128]{3,2,1,0:T(8,128)S(1)}, f32[2,8,8,128]{3,2,1,0:T(8,128)}, u32[]{:S(2)}) copy-start(f32[2,8,8,128]{3,2,1,0:T(8,128)} %param.9) | copy-start | bytes 196612
  1.7 0.8 %copy-start.4 = (f32[2,8,8,128]{3,2,1,0:T(8,128)S(1)}, f32[2,8,8,128]{3,2,1,0:T(8,128)}, u32[]{:S(2)}) copy-start(f32[2,8,8,128]{3,2,1,0:T(8,128)} %param.10) | copy-start | bytes 196612
  2.6 0.8 %copy-start.6 = (f32[2,8,8,128]{3,2,1,0:T(8,128)S(1)}, f32[2,8,8,128]{3,2,1,0:T(8,128)}, u32[]{:S(2)}) copy-start(f32[2,8,8,128]{3,2,1,0:T(8,128)} %param.8) | copy-start | bytes 196612
  3.4 0.7 %copy-start.7 = (f32[2]{0:T(128)S(1)}, f32[2]{0:T(128)}, u32[]{:S(2)}) copy-start(f32[2]{0:T(128)} %step_ref.5) | copy-start | bytes 28
  4.8 6.4 %collective-permute-start.1 = (bf16[2,16,128]{2,1,0:T(8,128)(2,1)S(1)}, bf16[2,16,128]{2,1,0:T(8,128)(2,1)S(1)}, u32[]{:S(2)}, u32[]{:S(2)}) collective-permute-start(bf16[2,16,128]{2,1,0:T(8,128)(2,1)S(1)} %get-tuple-element.14), channel_id=1, source_target_pairs={{0,1},{1,0},{2,3},{3,2},{4,5},{5,4},{6,7},{7,6},{8,9},{9,8},{10,11... | collective-permute-start | bytes 24584 | tf_op jit(solution)/shard_map/ppermute | solution.py:295
  5.3 5.8 %collective-permute-start.2 = (bf16[2,16,128]{2,1,0:T(8,128)(2,1)S(1)}, bf16[2,16,128]{2,1,0:T(8,128)(2,1)S(1)}, u32[]{:S(2)}, u32[]{:S(2)}) collective-permute-start(bf16[2,16,128]{2,1,0:T(8,128)(2,1)S(1)} %get-tuple-element.15), channel_id=1, source_target_pairs={{0,3},{1,2},{2,1},{3,0},{4,7},{5,6},{6,5},{7,4},{8,11},{9,10},{10,... | collective-permute-start | bytes 24584 | tf_op jit(solution)/shard_map/ppermute | solution.py:295
  7.9 3.8 %collective-permute-start = (bf16[6,16,128]{2,1,0:T(8,128)(2,1)S(1)}, bf16[6,16,128]{2,1,0:T(8,128)(2,1)S(1)}, u32[]{:S(2)}, u32[]{:S(2)}) collective-permute-start(bf16[6,16,128]{2,1,0:T(8,128)(2,1)S(1)} %get-tuple-element.12), channel_id=1, source_target_pairs={{0,2},{2,0},{1,3},{3,1},{4,6},{6,4},{5,7},{7,5},{8,10},{10,8},{9,1... | collective-permute-start | bytes 73736 | tf_op jit(solution)/shard_map/ppermute | solution.py:305
  10.5 0.7 %copy-start.9 = (bf16[8,96]{1,0:T(8,128)(2,1)S(1)}, bf16[8,96]{1,0:T(8,128)(2,1)}, u32[]{:S(2)}) copy-start(bf16[8,96]{1,0:T(8,128)(2,1)} %param.15) | copy-start | bytes 4612
  10.5 8.0 %copy-start.8 = (f32[2]{0:T(128)S(1)}, f32[2]{0:T(128)}, u32[]{:S(2)}) copy-start(f32[2]{0:T(128)} %step_ref.5) | copy-start | bytes 28
  10.6 20.8 %copy-start.1 = (f32[2,2,8,8,128]{4,3,2,1,0:T(8,128)S(1)}, f32[2,2,8,8,128]{4,3,2,1,0:T(8,128)}, u32[]{:S(2)}) copy-start(f32[2,2,8,8,128]{4,3,2,1,0:T(8,128)} %param.11) | copy-start | bytes 393220
  10.6 20.8 %copy-start.3 = (f32[2,8,8,128]{3,2,1,0:T(8,128)S(1)}, f32[2,8,8,128]{3,2,1,0:T(8,128)}, u32[]{:S(2)}) copy-start(f32[2,8,8,128]{3,2,1,0:T(8,128)} %param.9) | copy-start | bytes 196612
  10.7 20.8 %copy-start.5 = (f32[2,8,8,128]{3,2,1,0:T(8,128)S(1)}, f32[2,8,8,128]{3,2,1,0:T(8,128)}, u32[]{:S(2)}) copy-start(f32[2,8,8,128]{3,2,1,0:T(8,128)} %param.10) | copy-start | bytes 196612
  11.8 6.6 %collective-permute-start.3 = (bf16[17,16,128]{2,1,0:T(8,128)(2,1)S(1)}, bf16[17,16,128]{2,1,0:T(8,128)(2,1)S(1)}, u32[]{:S(2)}, u32[]{:S(2)}) collective-permute-start(bf16[17,16,128]{2,1,0:T(8,128)(2,1)S(1)} %pad_maximum_fusion.own), channel_id=1, source_target_pairs={{0,4},{4,8},{8,12},{12,0},{1,5},{5,9},{9,13},{13,1},{2,6},{6,10},{... | collective-permute-start | bytes 208904 | tf_op jit(solution)/shard_map/ppermute | solution.py:329
  13.4 5.1 %collective-permute-start.4 = (bf16[17,16,128]{2,1,0:T(8,128)(2,1)S(1)}, bf16[17,16,128]{2,1,0:T(8,128)(2,1)S(1)}, u32[]{:S(2)}, u32[]{:S(2)}) collective-permute-start(bf16[17,16,128]{2,1,0:T(8,128)(2,1)S(1)} %pad_maximum_fusion.own), channel_id=1, source_target_pairs={{0,12},{4,0},{8,4},{12,8},{1,13},{5,1},{9,5},{13,9},{2,14},{6,2},{... | collective-permute-start | bytes 208904 | tf_op jit(solution)/shard_map/ppermute | solution.py:330
  25.4 6.0 %collective-permute-start.5 = (bf16[13,16,128]{2,1,0:T(8,128)(2,1)S(1)}, bf16[13,16,128]{2,1,0:T(8,128)(2,1)S(1)}, u32[]{:S(2)}, u32[]{:S(2)}) collective-permute-start(bf16[13,16,128]{2,1,0:T(8,128)(2,1)S(1)} %get-tuple-element.17.own), channel_id=1, source_target_pairs={{0,4},{4,8},{8,12},{12,0},{1,5},{5,9},{9,13},{13,1},{2,6},{6,10},{... | collective-permute-start | bytes 159752 | tf_op jit(solution)/shard_map/ppermute | solution.py:329
  26.5 4.9 %collective-permute-start.6 = (bf16[13,16,128]{2,1,0:T(8,128)(2,1)S(1)}, bf16[13,16,128]{2,1,0:T(8,128)(2,1)S(1)}, u32[]{:S(2)}, u32[]{:S(2)}) collective-permute-start(bf16[13,16,128]{2,1,0:T(8,128)(2,1)S(1)} %get-tuple-element.17.own), channel_id=1, source_target_pairs={{0,12},{4,0},{8,4},{12,8},{1,13},{5,1},{9,5},{13,9},{2,14},{6,2},{... | collective-permute-start | bytes 159752 | tf_op jit(solution)/shard_map/ppermute | solution.py:330

commit v3 on v2

--- a/solution.py
+++ b/solution.py
@@ -10,6 +10,12 @@
 LANES = 128
 REACH = 4
 EDGE = 2 * REACH
+GUARD = 8
+SLABS = 8
+SUMS = 4
+AHEAD = 2
+LIFT_ROWS = 2
+CHUNK = 7
 GRANT = 24 << 20
 BF = jnp.bfloat16
 F32 = jnp.float32
@@ -29,11 +35,22 @@
 
 
 def pack_kernel(
-    geometry, step_ref, prior, observed, weight, noise,
+    geometry, step_in, prior_in, observed_in, weight_in, noise_in,
     state_out, base_out, lon_out, *rest,
 ):
     frames, chans, rows, single = geometry
-    *outs, state, base = rest
+    *outs, state, base, prior, observed, weight, noise, step_ref, done = rest
+    size = frames * chans * rows
+    copies = [
+        pltpu.make_async_copy(source.at[:size], target, done.at[index])
+        for index, (source, target) in enumerate(
+            ((prior_in, prior), (observed_in, observed), (weight_in, weight), (noise_in, noise))
+        )
+    ] + [pltpu.make_async_copy(step_in, step_ref, done.at[4])]
+    for copy in copies:
+        copy.start()
+    for copy in copies:
+        copy.wait()
     step = step_ref[0]
     spread = jnp.sqrt(jnp.full((chans, LANES), 2.0 * step, F32))
     for row in range(rows):
@@ -67,29 +84,38 @@
             edge_out[place] = tile.astype(BF)
 
 
-def features(geometry, in_rows, own, prev, following, lift, act, halo):
+def features(geometry, in_rows, own, prev, following, lift, act, slabs, turned, lifted):
     frames, ring = geometry
-    dims = (((0,), (0,)), ((), ()))
-
-    def lifted(tile):
-        stacked = jnp.concatenate([prev[tile], own[tile], following[tile]], axis=0)
-        turned = jnp.transpose(stacked.astype(F32)).astype(BF)
-        return jnp.dot(turned, lift[0], preferred_element_type=F32) + jnp.dot(
-            turned, lift[1], preferred_element_type=F32
+    for tile in range(in_rows + 1):
+        stacked = jnp.concatenate([prev[tile], own[tile], following[tile]] * 2, axis=0)
+        turned[tile * LANES : (tile + 1) * LANES, :] = jnp.transpose(stacked.astype(F32)).astype(BF)
+    halo = in_rows * LANES
+    lifted[...] = jnp.dot(turned[halo:, :], lift[...], preferred_element_type=F32)
+    for first in range(0, in_rows, LIFT_ROWS):
+        count = min(LIFT_ROWS, in_rows - first)
+        low = first * LANES
+        block = jnp.dot(
+            turned[low : low + count * LANES, :], lift[...], preferred_element_type=F32
         )
-
-    halo[...] = lifted(in_rows)
-    for row in range(in_rows):
-        main = lifted(row)
-        whole = jnp.concatenate([main, halo[row * EDGE : (row + 1) * EDGE, :]], axis=0)
-        for frame in range(frames):
-            store_shifts(act, frame, row, ring, whole[:, frame * LANES : (frame + 1) * LANES])
-
-
-def store_shifts(act, frame, row, ring, value):
-    act[0, frame, row, :ring, :] = pltpu.roll(value, 1, 0).astype(BF)
+        for row in range(first, first + count):
+            for frame in range(frames):
+                part = slice(frame * LANES, (frame + 1) * LANES)
+                start = (row - first) * LANES
+                value = jnp.concatenate(
+                    [block[start : start + LANES, part], lifted[row * EDGE : (row + 1) * EDGE, part]],
+                    axis=0,
+                )
+                store_shifts(act, slabs[(2 * row + frame) % SLABS], frame, row, ring, value)
+
+
+def store_shifts(act, slab, frame, row, ring, value):
+    at = GUARD
+    slab[at : at + ring, :] = value
+    slab[at - 1 : at, :] = value[ring - 1 :]
+    slab[at + ring : at + ring + 1, :] = value[:1]
+    act[0, frame, row, :ring, :] = slab[at - 1 : at - 1 + ring, :].astype(BF)
     act[1, frame, row, :ring, :] = value.astype(BF)
-    act[2, frame, row, :ring, :] = pltpu.roll(value, ring - 1, 0).astype(BF)
+    act[2, frame, row, :ring, :] = slab[at + 1 : at + 1 + ring, :].astype(BF)
 
 
 def conv_pairs(act, frame, weight, first, count):
@@ -105,32 +131,44 @@
     return half + half * jnp.tanh(half)
 
 
-def convolve(geometry, in_rows, reach, act, act2, sums, conv_a, conv_b, top, bottom, emit):
+def convolve(
+    geometry, in_rows, reach, act, act2, slabs, sums, conv_a, conv_b, top, bottom, emit
+):
     frames, ring, pad, chunk = geometry
-    for frame in range(frames):
-        pairs = (in_rows - 2) // 2
-        for first in range(0, pairs, chunk):
-            count = min(chunk, pairs - first)
-            sums[: count * pad, :] = conv_pairs(act, frame, conv_a, first, count)
-            for p in range(count):
-                for q in range(2):
-                    row = 1 + 2 * (first + p) + q
-                    value = gated(sums[p * pad : p * pad + ring, q * LANES : (q + 1) * LANES])
-                    if row < reach:
-                        value = value * top
-                    if row >= in_rows - reach:
-                        value = value * bottom
-                    store_shifts(act2, frame, row - 1, ring, value)
-        pairs = (in_rows - 4) // 2
-        for first in range(0, pairs, chunk):
-            count = min(chunk, pairs - first)
-            sums[: count * pad, :] = conv_pairs(act2, frame, conv_b, first, count)
-            for p in range(count):
-                for q in range(2):
-                    row = 2 + 2 * (first + p) + q
-                    value = gated(sums[p * pad : p * pad + ring, q * LANES : (q + 1) * LANES])
-                    merged = act[1, frame, row, :ring, :].astype(F32) + value
-                    emit(frame, row - 2, merged)
+    waiting = []
+
+    def finish():
+        into, frame, first, count, place = waiting.pop(0)
+        for p in range(count):
+            for q in range(2):
+                row = 2 * (first + p) + q
+                value = gated(into[p * pad : p * pad + ring, q * LANES : (q + 1) * LANES])
+                if place == 2:
+                    merged = act[1, frame, row + 2, :ring, :].astype(F32) + value
+                    emit(frame, row, merged)
+                    continue
+                if row + 1 < reach:
+                    value = value * top
+                if row + 1 >= in_rows - reach:
+                    value = value * bottom
+                store_shifts(act2, slabs[row % SLABS], frame, row, ring, value)
+
+    used = 0
+    for place, source, weight in ((1, act, conv_a), (2, act2, conv_b)):
+        pairs = (in_rows - 2 * place) // 2
+        for frame in range(frames):
+            for first in range(0, pairs, chunk):
+                count = min(chunk, pairs - first)
+                while any(w[4] < place and w[1] == frame for w in waiting):
+                    finish()
+                into = sums[used % len(sums)]
+                used += 1
+                into[: count * pad, :] = conv_pairs(source, frame, weight, first, count)
+                waiting.append((into, frame, first, count, place))
+                if len(waiting) > AHEAD:
+                    finish()
+    while waiting:
+        finish()
 
 
 def edge_flags():
@@ -148,13 +186,14 @@
 
 def first_kernel(
     geometry, step_ref, own, prev, following, base, base_edge, lift, conv_a, conv_b, out_weight,
-    next_out, state_out, act, act2, sums, halo, halo_merged,
+    next_out, state_out, act, act2, turned, lifted, halo_merged, *rest,
 ):
+    slabs, sums = rest[:SLABS], rest[SLABS:]
     frames, chans, rows, ring, pad, chunk = geometry
     in_rows, out_rows = rows + 2 * REACH, rows + 4
     top, bottom = edge_flags()
     step = step_ref[0]
-    features((frames, ring), in_rows, own, prev, following, lift, act, halo)
+    features((frames, ring), in_rows, own, prev, following, lift, act, slabs, turned, lifted)
 
     def emit(frame, row, merged):
         score = project(out_weight, merged[:LANES].astype(BF))
@@ -174,7 +213,8 @@
         halo_merged[frame, row * EDGE : (row + 1) * EDGE, :] = merged[LANES:]
 
     convolve(
-        (frames, ring, pad, chunk), in_rows, REACH, act, act2, sums, conv_a, conv_b, top, bottom, emit
+        (frames, ring, pad, chunk), in_rows, REACH, act, act2, slabs, sums, conv_a, conv_b,
+        top, bottom, emit,
     )
     for row in range(out_rows):
         next_out[row] = state_out[row].astype(BF)
@@ -190,14 +230,15 @@
 
 def last_kernel(
     geometry, step_ref, own, prev, following, state, observed, weight, noise, lift, conv_a, conv_b,
-    out_weight, result, act, act2, sums, halo,
+    out_weight, result, act, act2, turned, lifted, *rest,
 ):
+    slabs, sums = rest[:SLABS], rest[SLABS:]
     frames, chans, rows, ring, pad, chunk = geometry
     in_rows = rows + 4
     top, bottom = edge_flags()
     step = step_ref[1]
     spread = jnp.sqrt(jnp.full((chans, LANES), 2.0 * step, F32))
-    features((frames, ring), in_rows, own, prev, following, lift, act, halo)
+    features((frames, ring), in_rows, own, prev, following, lift, act, slabs, turned, lifted)
 
     def emit(frame, row, merged):
         score = project(out_weight, merged[:LANES].astype(BF))
@@ -210,7 +251,10 @@
             + spread * noise[late, :]
         )
 
-    convolve((frames, ring, pad, chunk), in_rows, 2, act, act2, sums, conv_a, conv_b, top, bottom, emit)
+    convolve(
+        (frames, ring, pad, chunk), in_rows, 2, act, act2, slabs, sums, conv_a, conv_b, top, bottom,
+        emit,
+    )
 
 
 def ring_perm(count, by):
@@ -238,7 +282,7 @@
     )
     lift = lift * kept
     high = lax.reduce_precision(lift, 8, 7)
-    lift = jnp.stack([high.astype(BF), (lift - high).astype(BF)])
+    lift = jnp.concatenate([high, lift - high], axis=0).astype(BF)
     half = conv_weights * jnp.asarray(0.5, BF)
     taps = jnp.swapaxes(half, 2, 3).reshape(2, 3, 3, hidden, hidden)
     taps = jnp.pad(taps, ((0, 0), (0, 0), (0, 0), (0, gap), (0, gap)))
@@ -259,7 +303,7 @@
     frames, chans, rows, cols = prior_state.shape
     lat_count, lon_count = lax.axis_size("lat"), lax.axis_size("lon")
     fc = frames * chans
-    ring, pad, chunk = cols + EDGE, cols + 16, 4
+    ring, pad, chunk = cols + EDGE, cols + 16, CHUNK
     smem = pl.BlockSpec(memory_space=pltpu.SMEM)
     vmem = pl.BlockSpec(memory_space=pltpu.VMEM)
     shape = jax.ShapeDtypeStruct
@@ -276,11 +320,23 @@
             shape((2, fc, cols), BF),
             *sides,
         ),
-        in_specs=[smem] + [vmem] * 4,
+        in_specs=[pl.BlockSpec(memory_space=pltpu.HBM)] * 5,
         out_specs=[vmem] * (3 + len(sides)),
-        scratch_shapes=[pltpu.VMEM((rows, fc, cols), F32), pltpu.VMEM((rows, fc, cols), F32)],
+        scratch_shapes=[
+            *[pltpu.VMEM((rows, fc, cols), F32)] * 2,
+            *[pltpu.VMEM((fc * rows, cols), F32)] * 4,
+            pltpu.SMEM(step_sizes.shape, F32),
+            pltpu.SemaphoreType.DMA((5,)),
+        ],
         compiler_params=pltpu.CompilerParams(vmem_limit_bytes=GRANT),
-    )(step_sizes, flat(prior_state), flat(observed), flat(obs_weight), noise_field.reshape(-1, cols))
+    )(
+        *[
+            pltpu.with_memory_space_constraint(array, pltpu.HBM)
+            for array in (
+                step_sizes, flat(prior_state), flat(observed), flat(obs_weight), noise_field.reshape(-1, cols)
+            )
+        ],
+    )
 
     lat = lax.axis_index("lat")
     spot = ("lat", "lon")
@@ -321,6 +377,7 @@
     own = jnp.concatenate([from_top[:REACH], state, from_bottom[:REACH], edge[:1]], axis=0)
     base_edge = jnp.concatenate([from_top[REACH:], from_bottom[REACH:], edge[1:]], axis=0)
 
+    conv_weights, own = lax.optimization_barrier((conv_weights, own))
     lift, conv_a, conv_b, out_lanes = lane_weights(lift_weight, conv_weights, out_weight)
     tm_count = lax.axis_size("tm")
 
@@ -332,12 +389,15 @@
 
     geometry = (frames, chans, rows, ring, pad, chunk)
 
-    def scratch(in_rows):
+    def scratch(in_rows, *more):
         return [
             pltpu.VMEM((3, frames, in_rows, pad, LANES), BF),
             pltpu.VMEM((3, frames, in_rows - 2, pad, LANES), BF),
-            pltpu.VMEM((chunk * pad, 2 * LANES), F32),
+            pltpu.VMEM(((in_rows + 1) * LANES, 6 * fc), BF),
             pltpu.VMEM((LANES, 2 * LANES), F32),
+            *more,
+            *[pltpu.VMEM((ring + 2 * GUARD, LANES), F32)] * SLABS,
+            *[pltpu.VMEM((chunk * pad, 2 * LANES), F32)] * SUMS,
         ]
 
     prev, following = neighbours(own)
@@ -346,7 +406,7 @@
         out_shape=(shape((rows + 5, fc, cols), BF), shape((rows + 4, fc, cols), F32)),
         in_specs=[smem] + [vmem] * 9,
         out_specs=[vmem] * 2,
-        scratch_shapes=scratch(rows + 2 * REACH) + [pltpu.VMEM((frames, LANES, LANES), F32)],
+        scratch_shapes=scratch(rows + 2 * REACH, pltpu.VMEM((frames, LANES, LANES), F32)),
         compiler_params=pltpu.CompilerParams(vmem_limit_bytes=GRANT),
     )(step_sizes, own, prev, following, base, base_edge, lift, conv_a, conv_b, out_lanes)
 

time: 37.9 us -> 30.5 us (0.80)
  local copies, waits for them, and re-layouts: 5.75 us -> 1.24 us
  Pallas kernels: 13.7 us -> 10.4 us
  other arithmetic: 1.47 us -> 2.27 us
    unnamed x20 -> x8, local copies, waits for them, and re-layouts: 4.36 us -> 0.03 us
    ppermute x2, waiting for transfers between devices: 4.88 us -> 2.91 us  [neighbours(): lax.ppermute(array, 'tm', ring_perm(tm_count, 1))]
    pallas_call x1, Pallas kernels: 6.88 us -> 4.93 us  [per_device(): pl.pallas_call(functools.partial(first_kernel, geometry), out_shape=(shap...]
    pallas_call x1, Pallas kernels: 6.1 us -> 4.32 us  [per_device(): pl.pallas_call(functools.partial(last_kernel, geometry), out_shape=shape(...]
    ppermute x1, waiting for transfers between devices: 0.56 us -> 2.07 us  [per_device(): rows_in = lax.ppermute(outward[0], 'lat', ring_perm(2, 1))]
    another operation x1, other arithmetic: 0.01 us -> 0.88 us  [lane_weights(): lift = jnp.stack([high.astype(BF), (lift - high).astype(BF)])]
    concatenate x1 -> x0, local copies, waits for them, and re-layouts: 0.81 us -> none  [lane_weights(): lift = jnp.concatenate(lanes, axis=1)]
    pad x1, local copies, waits for them, and re-layouts: 0.01 us -> 0.69 us  [lane_weights(): return (lift, conv[0], conv[1], jnp.pad(out_weight, ((0, 0), (0, gap))))]
  transfers between devices with their start and end apart: 7 -> 7, of which waited for: 4 -> 4; matrix products, arithmetic and copies ran while one was open for 8% -> 11% of each run, Pallas kernels for 0% -> 0%
where the time goes in v3:
time: 30.5 us; the launch traced here: 30.2 us
  starting transfers between devices  10.9 us (36%)
  Pallas kernels  10.4 us (34%)
  waiting for transfers between devices  5.18 us (17%)
  other arithmetic  2.27 us (7%)
  local copies, waits for them, and re-layouts  1.24 us (4%)
    ppermute x2, starting transfers between devices, neighbours(): lax.ppermute(array, 'tm', ring_perm(tm_count, -1))  5.06 us
    pallas_call x1, Pallas kernels, per_device(): pl.pallas_call(functools.partial(first_kernel, geometry), out_shape=(shap...  4.93 us
    pallas_call x1, Pallas kernels, per_device(): pl.pallas_call(functools.partial(last_kernel, geometry), out_shape=shape(...  4.32 us
    ppermute x2, starting transfers between devices, move(): return lax.ppermute(array, spot, perm)  3.15 us
    ppermute x2, waiting for transfers between devices, neighbours(): lax.ppermute(array, 'tm', ring_perm(tm_count, 1))  2.91 us
    ppermute x2, starting transfers between devices, neighbours(): lax.ppermute(array, 'tm', ring_perm(tm_count, 1))  2.69 us
    ppermute x1, waiting for transfers between devices, per_device(): rows_in = lax.ppermute(outward[0], 'lat', ring_perm(2, 1))  2.07 us
    pallas_call x1, Pallas kernels, per_device(): pl.pallas_call(functools.partial(pack_kernel, (frames, chans, rows, lat_c...  1.13 us
  transfers between devices with their start and end apart: 7, of which 4 were waited for; matrix products, arithmetic and copies ran while one was open for 11% of the time, Pallas kernels for 0%

profile of v3, /device:TPU:0, one launch (start us, length us, event | category | flops | bytes accessed | tf_op | source)
XLA Modules:
  0.0 30.2 jit_solution(1896499975510298603)
XLA Ops:
  0.0 1.1 %shard_map.82 = (bf16[8,16,128]{2,1,0:T(8,128)(2,1)S(1)}, f32[8,16,128]{2,1,0:T(8,128)S(1)}, bf16[2,16,128]{2,1,0:T(8,128)(2,1)S(1)}, bf16[6,16,128]{2,1,0:T(8,128)(2,1)S(1)}, bf16[2,16,128]{2,1,0:T(8,128)(2,1)S(1)}) custom-call(f32[2]{0:T(128)} %step_ref.3, f32[128,128]{1,0:T(8,128)} %bitcast.34, f32[128,128]{1,0:T(8,128)} %bitcast.29, ...), custom_call_target="tpu_custom_call" | custom-call | tf_op jit(solution)/shard_map/pallas_call | solution.py:315
  1.1 0.6 %collective-permute-start.1 = (bf16[2,16,128]{2,1,0:T(8,128)(2,1)S(1)}, bf16[2,16,128]{2,1,0:T(8,128)(2,1)S(1)}, u32[]{:S(2)}, u32[]{:S(2)}) collective-permute-start(bf16[2,16,128]{2,1,0:T(8,128)(2,1)S(1)} %get-tuple-element.16), channel_id=1, source_target_pairs={{0,1},{1,0},{2,3},{3,2},{4,5},{5,4},{6,7},{7,6},{8,9},{9,8},{10,11... | collective-permute-start | bytes 24584 | tf_op jit(solution)/shard_map/ppermute | solution.py:351
  1.7 2.6 %collective-permute-start.2 = (bf16[2,16,128]{2,1,0:T(8,128)(2,1)S(1)}, bf16[2,16,128]{2,1,0:T(8,128)(2,1)S(1)}, u32[]{:S(2)}, u32[]{:S(2)}) collective-permute-start(bf16[2,16,128]{2,1,0:T(8,128)(2,1)S(1)} %get-tuple-element.17), channel_id=1, source_target_pairs={{0,3},{1,2},{2,1},{3,0},{4,7},{5,6},{6,5},{7,4},{8,11},{9,10},{10,... | collective-permute-start | bytes 24584 | tf_op jit(solution)/shard_map/ppermute | solution.py:351
  4.3 0.0 collective-permute-start
  4.3 0.1 fusion.5
  4.4 0.9 %reduce-precision_convert_fusion = (bf16[48,256]{1,0:T(8,128)(2,1)S(1)}, bf16[48,256]{1,0:T(8,128)(2,1)S(1)}) fusion(f32[40,96]{1,0:T(8,128)} %bitcast.35, f32[48]{0:T(128)S(1)} %fusion.5), kind=kLoop, calls=%fused_computation.7 | loop fusion | flops 122880 | bytes 64704 | tf_op jit(solution)/shard_map/convert
  5.3 0.7 %pad.29.out_weight = bf16[8,128]{1,0:T(8,128)(2,1)S(1)} pad(bf16[8,96]{1,0:T(8,128)(2,1)} %param.15, bf16[]{:T(256)} %constant.8.clone.1), padding=0_0x0_32 | pad | bytes 3586 | tf_op jit(solution)/shard_map/jit(_pad)/pad | solution.py:297
  6.0 0.0 collective-permute-done.1
  6.0 0.0 collective-permute-done.2
  6.0 2.1 %collective-permute-done = bf16[6,16,128]{2,1,0:T(8,128)(2,1)S(1)} collective-permute-done((bf16[6,16,128]{2,1,0:T(8,128)(2,1)S(1)}, bf16[6,16,128]{2,1,0:T(8,128)(2,1)S(1)}, u32[]{:S(2)}, u32[]{:S(2)}) %collective-permute-start) | collective-permute-done | bytes 24608 | tf_op jit(solution)/shard_map/ppermute | solution.py:361
  8.2 1.6 %collective-permute-start.3 = (bf16[17,16,128]{2,1,0:T(8,128)(2,1)S(1)}, bf16[17,16,128]{2,1,0:T(8,128)(2,1)S(1)}, u32[]{:S(2)}, u32[]{:S(2)}) collective-permute-start(bf16[17,16,128]{2,1,0:T(8,128)(2,1)S(1)} %pad_maximum_fusion.own), channel_id=1, source_target_pairs={{0,4},{4,8},{8,12},{12,0},{1,5},{5,9},{9,13},{13,1},{2,6},{6,10},{... | collective-permute-start | bytes 208904 | tf_op jit(solution)/shard_map/ppermute | solution.py:386
  9.8 2.2 %collective-permute-start.4 = (bf16[17,16,128]{2,1,0:T(8,128)(2,1)S(1)}, bf16[17,16,128]{2,1,0:T(8,128)(2,1)S(1)}, u32[]{:S(2)}, u32[]{:S(2)}) collective-permute-start(bf16[17,16,128]{2,1,0:T(8,128)(2,1)S(1)} %pad_maximum_fusion.own), channel_id=1, source_target_pairs={{0,12},{4,0},{8,4},{12,8},{1,13},{5,1},{9,5},{13,9},{2,14},{6,2},{... | collective-permute-start | bytes 208904 | tf_op jit(solution)/shard_map/ppermute | solution.py:387
  12.0 1.1 %broadcast_multiply_fusion = bf16[2,9,96,96]{3,2,1,0:T(8,128)(2,1)S(1)} fusion(bf16[2,9,96,96]{3,2,1,0:T(8,128)(2,1)} %param.14), kind=kLoop, calls=%fused_computation.5 | loop fusion | flops 165888 | bytes 663552 | tf_op jit(solution)/shard_map/mul | solution.py:286
  13.1 0.3 copy.9
  13.4 0.2 pad.26
  13.5 0.2 fusion.2
  13.7 0.0 copy-start.3
  13.7 0.1 fusion.6
  13.9 0.0 copy-start
  13.9 0.0 copy-start.1
  13.9 0.0 copy-start.2
  13.9 0.7 %collective-permute-done.3.prev = bf16[17,16,128]{2,1,0:T(8,128)(2,1)S(1)} collective-permute-done((bf16[17,16,128]{2,1,0:T(8,128)(2,1)S(1)}, bf16[17,16,128]{2,1,0:T(8,128)(2,1)S(1)}, u32[]{:S(2)}, u32[]{:S(2)}) %collective-permute-start.3) | collective-permute-done | bytes 69664 | tf_op jit(solution)/shard_map/ppermute | solution.py:386
  14.7 0.2 collective-permute-done.4.following
  14.9 0.0 copy-done.3
  14.9 4.9 %shard_map.83 = (bf16[13,16,128]{2,1,0:T(8,128)(2,1)S(1)}, f32[12,16,128]{2,1,0:T(8,128)S(1)}) custom-call(f32[2]{0:T(128)S(1)} %copy-done.3, bf16[17,16,128]{2,1,0:T(8,128)(2,1)S(1)} %pad_maximum_fusion.own, bf16[17,16,128]{2,1,0:T(8,128)(2,1)S(1)} %collective-permute-done.3.prev, bf16[17,16,128]{2,1,0:T(8,128)(2,1)S(1)} %collective-permute-done.4.following, ...), custom_call_target="tpu_custom_call" | custom-call | tf_op jit(solution)/shard_map/pallas_call | solution.py:404
  19.8 1.1 %collective-permute-start.5 = (bf16[13,16,128]{2,1,0:T(8,128)(2,1)S(1)}, bf16[13,16,128]{2,1,0:T(8,128)(2,1)S(1)}, u32[]{:S(2)}, u32[]{:S(2)}) collective-permute-start(bf16[13,16,128]{2,1,0:T(8,128)(2,1)S(1)} %get-tuple-element.21.own), channel_id=1, source_target_pairs={{0,4},{4,8},{8,12},{12,0},{1,5},{5,9},{9,13},{13,1},{2,6},{6,10},{... | collective-permute-start | bytes 159752 | tf_op jit(solution)/shard_map/ppermute | solution.py:386
  20.8 2.8 %collective-permute-start.6 = (bf16[13,16,128]{2,1,0:T(8,128)(2,1)S(1)}, bf16[13,16,128]{2,1,0:T(8,128)(2,1)S(1)}, u32[]{:S(2)}, u32[]{:S(2)}) collective-permute-start(bf16[13,16,128]{2,1,0:T(8,128)(2,1)S(1)} %get-tuple-element.21.own), channel_id=1, source_target_pairs={{0,12},{4,0},{8,4},{12,8},{1,13},{5,1},{9,5},{13,9},{2,14},{6,2},{... | collective-permute-start | bytes 159752 | tf_op jit(solution)/shard_map/ppermute | solution.py:387
  23.7 2.2 %collective-permute-done.5.prev = bf16[13,16,128]{2,1,0:T(8,128)(2,1)S(1)} collective-permute-done((bf16[13,16,128]{2,1,0:T(8,128)(2,1)S(1)}, bf16[13,16,128]{2,1,0:T(8,128)(2,1)S(1)}, u32[]{:S(2)}, u32[]{:S(2)}) %collective-permute-start.5) | collective-permute-done | bytes 53280 | tf_op jit(solution)/shard_map/ppermute | solution.py:386
  25.8 0.0 collective-permute-done.6.following
  25.8 0.0 copy-done
  25.8 0.0 copy-done.1
  25.8 0.0 copy-done.2
  25.8 4.3 %shard_map.84 = f32[128,128]{1,0:T(8,128)} custom-call(f32[2]{0:T(128)S(1)} %copy-done.3, bf16[13,16,128]{2,1,0:T(8,128)(2,1)S(1)} %get-tuple-element.21.own, bf16[13,16,128]{2,1,0:T(8,128)(2,1)S(1)} %collective-permute-done.5.prev, bf16[13,16,128]{2,1,0:T(8,128)(2,1)S(1)} %collective-permute-done.6.following, f32[12,16,128]{2,1,0:T(8,128)S(1)} %get-tuple-element.22.state, ...), custom_call_target="tpu_custom_call" | custom-call | tf_op jit(solution)/shard_map/pallas_call | solution.py:414
  (13 shorter events, 0.1 us)
Async XLA Ops:
  1.1 4.9 %collective-permute-start.1 = (bf16[2,16,128]{2,1,0:T(8,128)(2,1)S(1)}, bf16[2,16,128]{2,1,0:T(8,128)(2,1)S(1)}, u32[]{:S(2)}, u32[]{:S(2)}) collective-permute-start(bf16[2,16,128]{2,1,0:T(8,128)(2,1)S(1)} %get-tuple-element.16), channel_id=1, source_target_pairs={{0,1},{1,0},{2,3},{3,2},{4,5},{5,4},{6,7},{7,6},{8,9},{9,8},{10,11... | collective-permute-start | bytes 24584 | tf_op jit(solution)/shard_map/ppermute | solution.py:351
  1.7 4.3 %collective-permute-start.2 = (bf16[2,16,128]{2,1,0:T(8,128)(2,1)S(1)}, bf16[2,16,128]{2,1,0:T(8,128)(2,1)S(1)}, u32[]{:S(2)}, u32[]{:S(2)}) collective-permute-start(bf16[2,16,128]{2,1,0:T(8,128)(2,1)S(1)} %get-tuple-element.17), channel_id=1, source_target_pairs={{0,3},{1,2},{2,1},{3,0},{4,7},{5,6},{6,5},{7,4},{8,11},{9,10},{10,... | collective-permute-start | bytes 24584 | tf_op jit(solution)/shard_map/ppermute | solution.py:351
  4.3 3.8 %collective-permute-start = (bf16[6,16,128]{2,1,0:T(8,128)(2,1)S(1)}, bf16[6,16,128]{2,1,0:T(8,128)(2,1)S(1)}, u32[]{:S(2)}, u32[]{:S(2)}) collective-permute-start(bf16[6,16,128]{2,1,0:T(8,128)(2,1)S(1)} %get-tuple-element.14), channel_id=1, source_target_pairs={{0,2},{2,0},{1,3},{3,1},{4,6},{6,4},{5,7},{7,5},{8,10},{10,8},{9,1... | collective-permute-start | bytes 73736 | tf_op jit(solution)/shard_map/ppermute | solution.py:361
  8.2 6.5 %collective-permute-start.3 = (bf16[17,16,128]{2,1,0:T(8,128)(2,1)S(1)}, bf16[17,16,128]{2,1,0:T(8,128)(2,1)S(1)}, u32[]{:S(2)}, u32[]{:S(2)}) collective-permute-start(bf16[17,16,128]{2,1,0:T(8,128)(2,1)S(1)} %pad_maximum_fusion.own), channel_id=1, source_target_pairs={{0,4},{4,8},{8,12},{12,0},{1,5},{5,9},{9,13},{13,1},{2,6},{6,10},{... | collective-permute-start | bytes 208904 | tf_op jit(solution)/shard_map/ppermute | solution.py:386
  9.8 5.1 %collective-permute-start.4 = (bf16[17,16,128]{2,1,0:T(8,128)(2,1)S(1)}, bf16[17,16,128]{2,1,0:T(8,128)(2,1)S(1)}, u32[]{:S(2)}, u32[]{:S(2)}) collective-permute-start(bf16[17,16,128]{2,1,0:T(8,128)(2,1)S(1)} %pad_maximum_fusion.own), channel_id=1, source_target_pairs={{0,12},{4,0},{8,4},{12,8},{1,13},{5,1},{9,5},{13,9},{2,14},{6,2},{... | collective-permute-start | bytes 208904 | tf_op jit(solution)/shard_map/ppermute | solution.py:387
  13.7 1.1 %copy-start.3 = (f32[2]{0:T(128)S(1)}, f32[2]{0:T(128)}, u32[]{:S(2)}) copy-start(f32[2]{0:T(128)} %step_ref.3) | copy-start | bytes 28
  13.9 12.0 %copy-start = (f32[2,2,8,8,128]{4,3,2,1,0:T(8,128)S(1)}, f32[2,2,8,8,128]{4,3,2,1,0:T(8,128)}, u32[]{:S(2)}) copy-start(f32[2,2,8,8,128]{4,3,2,1,0:T(8,128)} %param.11) | copy-start | bytes 393220
  13.9 11.9 %copy-start.1 = (f32[2,8,8,128]{3,2,1,0:T(8,128)S(1)}, f32[2,8,8,128]{3,2,1,0:T(8,128)}, u32[]{:S(2)}) copy-start(f32[2,8,8,128]{3,2,1,0:T(8,128)} %param.9) | copy-start | bytes 196612
  13.9 11.9 %copy-start.2 = (f32[2,8,8,128]{3,2,1,0:T(8,128)S(1)}, f32[2,8,8,128]{3,2,1,0:T(8,128)}, u32[]{:S(2)}) copy-start(f32[2,8,8,128]{3,2,1,0:T(8,128)} %param.10) | copy-start | bytes 196612
  19.8 6.0 %collective-permute-start.5 = (bf16[13,16,128]{2,1,0:T(8,128)(2,1)S(1)}, bf16[13,16,128]{2,1,0:T(8,128)(2,1)S(1)}, u32[]{:S(2)}, u32[]{:S(2)}) collective-permute-start(bf16[13,16,128]{2,1,0:T(8,128)(2,1)S(1)} %get-tuple-element.21.own), channel_id=1, source_target_pairs={{0,4},{4,8},{8,12},{12,0},{1,5},{5,9},{9,13},{13,1},{2,6},{6,10},{... | collective-permute-start | bytes 159752 | tf_op jit(solution)/shard_map/ppermute | solution.py:386
  20.8 5.0 %collective-permute-start.6 = (bf16[13,16,128]{2,1,0:T(8,128)(2,1)S(1)}, bf16[13,16,128]{2,1,0:T(8,128)(2,1)S(1)}, u32[]{:S(2)}, u32[]{:S(2)}) collective-permute-start(bf16[13,16,128]{2,1,0:T(8,128)(2,1)S(1)} %get-tuple-element.21.own), channel_id=1, source_target_pairs={{0,12},{4,0},{8,4},{12,8},{1,13},{5,1},{9,5},{13,9},{2,14},{6,2},{... | collective-permute-start | bytes 159752 | tf_op jit(solution)/shard_map/ppermute | solution.py:387
